TPU v7x, 32 devices: a whole 2x2x4 slice. The times are simulated.
32 devices in a mesh: groups: 2 (over y), blk: 4 (over z), rep: 2 (over x), sub: 2 (over core).
Axes of the slice: x: 2, y: 2, z: 4, core: 2. Of those that a mesh axis runs over, the one named last changes fastest.
Arguments:
- positions: float32 [3, 12288], P(None, ('groups', 'blk', 'rep', 'sub')), parts along dimension 1, may hold values from -19 to 19
- velocities: float32 [3, 12288], P(None, ('groups', 'blk', 'rep', 'sub')), parts along dimension 1, may hold values from -6 to 6
- charges: float32 [12288], P(('groups', 'blk', 'rep', 'sub')), parts along dimension 0, may hold values from -2.4 to 2.4
- dipoles: float32 [3, 12288], P(None, ('groups', 'blk', 'rep', 'sub')), parts along dimension 1, may hold values from -1.8 to 1.8
- quadrupoles: float32 [6, 12288], P(None, ('groups', 'blk', 'rep', 'sub')), parts along dimension 1, may hold values from -1.2 to 1.2
- damping: float32 [12288], P(('groups', 'blk', 'rep', 'sub')), parts along dimension 0, may hold values from 0.5 to 2
- inverse_mass: float32 [12288], P(('groups', 'blk', 'rep', 'sub')), parts along dimension 0, may hold values from 0.0625 to 1
- bonds: int32 [2, 12288], P(None, ('groups', 'blk', 'rep', 'sub')), parts along dimension 1, may hold values from 0 to 767
- bond_length: float32 [12288], P(('groups', 'blk', 'rep', 'sub')), parts along dimension 0, may hold values from 1 to 4
- angles: int32 [3, 24576], P(None, ('groups', 'blk', 'rep', 'sub')), parts along dimension 1, may hold values from 0 to 767
- torsions: int32 [4, 24576], P(None, ('groups', 'blk', 'rep', 'sub')), parts along dimension 1, may hold values from 0 to 767
Outputs:
- new_positions: float32 [3, 12288], P(None, ('groups', 'blk', 'rep', 'sub')), parts along dimension 1
- new_velocities: float32 [3, 12288], P(None, ('groups', 'blk', 'rep', 'sub')), parts along dimension 1
- slow_force: float32 [3, 12288], P(None, ('groups', 'blk', 'rep', 'sub')), parts along dimension 1
- slow_torque: float32 [3, 12288], P(None, ('groups', 'blk', 'rep', 'sub')), parts along dimension 1
There are 2 independent parts, one for each index of `groups`. A program takes and returns all parts, laid end to end along the dimension named above; each array names one. Nothing has to cross between parts.
Inputs may be any that keep to these rules, and one draw needn't show every extreme that they name: `bonds`: bond term k indexes atoms of domain k // 768, counted within it. `angles`: angle term k indexes atoms of domain k // 1536, counted within it. `torsions`: torsion term k indexes atoms of domain k // 1536, counted within it.
All inputs are finite; a program needn't handle non-finite values.
Results may differ from a plain program's by a relative error of at most 0.0003.
Values sent between devices are 32-bit elements; how exact they have to be, the bound alone decides.
A program may use at most 64 MiB of HBM per device.

v0:
```python
import math

import jax
import jax.numpy as jnp
from jax import lax
from jax.sharding import PartitionSpec as P

INNER = 4


QUAD_INDEX = ((0, 1, 2), (1, 3, 4), (2, 4, 5))
BOND_K = 0.3
ANGLE_K = 4.0
ANGLE_REST = -0.33
TORSION_K = 2.0
OUTER_DT = 0.2


def shifted(array, axis, by):
    count = lax.axis_size(axis)
    return lax.ppermute(array, axis, [(i, (i + by) % count) for i in range(count)])


def inner3(left, right):
    return left[0] * right[0] + left[1] * right[1] + left[2] * right[2]


def pair_energy(
    target_pos, target_dip, target_quad, target_charge, target_damp, source, target_ids, source_ids
):
    separation = [source[c][None, :] - target_pos[c][:, None] for c in range(3)]
    dist_sq = inner3(separation, separation) + target_damp[:, None] * source[13][None, :]
    inv_one = lax.rsqrt(dist_sq)
    inv_three = inv_one / dist_sq
    inv_five = 3.0 * inv_three / dist_sq
    inv_seven = 5.0 * inv_five / dist_sq
    inv_nine = 7.0 * inv_seven / dist_sq
    charge_i = target_charge[:, None]
    charge_k = source[3][None, :]
    dip_i = [target_dip[c][:, None] for c in range(3)]
    dip_k = [source[4 + c][None, :] for c in range(3)]
    quad_i = [[target_quad[QUAD_INDEX[a][b]][:, None] for b in range(3)] for a in range(3)]
    quad_k = [[source[7 + QUAD_INDEX[a][b]][None, :] for b in range(3)] for a in range(3)]
    quad_ir = [inner3(quad_i[a], separation) for a in range(3)]
    quad_kr = [inner3(quad_k[a], separation) for a in range(3)]
    dip_ir = inner3(dip_i, separation)
    dip_kr = inner3(dip_k, separation)
    dip_ik = inner3(dip_i, dip_k)
    quad_rri = inner3(quad_ir, separation)
    quad_rrk = inner3(quad_kr, separation)
    quad_rrik = inner3(quad_ir, quad_kr)
    quad_ik = sum((quad_i[a][b] * quad_k[a][b] for a in range(3) for b in range(3)))
    dip_iqk = inner3(dip_i, quad_kr)
    dip_kqi = inner3(dip_k, quad_ir)
    term_one = charge_i * charge_k
    term_two = charge_k * dip_ir - charge_i * dip_kr + dip_ik
    term_three = (
        charge_i * quad_rrk
        + charge_k * quad_rri
        - dip_ir * dip_kr
        + 2.0 * (dip_kqi - dip_iqk + quad_ik)
    )
    term_four = dip_ir * quad_rrk - dip_kr * quad_rri - 4.0 * quad_rrik
    term_five = quad_rri * quad_rrk
    energy = (
        term_one * inv_one
        + term_two * inv_three
        + term_three * inv_five
        + term_four * inv_seven
        + term_five * inv_nine
    )
    distinct = target_ids[:, None] != source_ids[None, :]
    return jnp.sum(jnp.where(distinct, energy, 0.0))


def pair_gradients(target, source, target_ids, source_ids):

    def tile_energy(target_pos, target_dip, target_quad):
        return pair_energy(
            target_pos,
            target_dip,
            target_quad,
            target[3],
            target[13],
            source,
            target_ids,
            source_ids,
        )

    grads = jax.grad(tile_energy, argnums=(0, 1, 2))(target[0:3], target[4:7], target[7:13])
    return jnp.concatenate(grads, 0)


def tile_gradients(targets, source, target_ids, source_ids):
    rows = targets.shape[1]
    width = math.gcd(rows, 256)
    blocks = rows // width
    target_blocks = targets.reshape(14, blocks, width).transpose(1, 0, 2)
    id_blocks = target_ids.reshape(blocks, width)

    def one_block(packed):
        return pair_gradients(packed[0], source, packed[1], source_ids)

    summed = lax.map(one_block, (target_blocks, id_blocks))
    return summed.transpose(1, 0, 2).reshape(12, rows)


def finish(partials, dipoles, quadrupoles):
    slow_force = -partials[0:3]
    field_dip = -partials[3:6]
    grad_quad = partials[6:12]
    halves = (1.0, 0.5, 0.5, 1.0, 0.5, 1.0)
    grad_matrix = [
        [halves[QUAD_INDEX[a][b]] * grad_quad[QUAD_INDEX[a][b]] for b in range(3)] for a in range(3)
    ]
    quad_matrix = [[quadrupoles[QUAD_INDEX[a][b]] for b in range(3)] for a in range(3)]
    product = [
        [
            quad_matrix[a][0] * grad_matrix[0][b]
            + quad_matrix[a][1] * grad_matrix[1][b]
            + quad_matrix[a][2] * grad_matrix[2][b]
            for b in range(3)
        ]
        for a in range(3)
    ]
    torque = jnp.stack(
        [
            dipoles[1] * field_dip[2]
            - dipoles[2] * field_dip[1]
            - 2.0 * (product[1][2] - product[2][1]),
            dipoles[2] * field_dip[0]
            - dipoles[0] * field_dip[2]
            - 2.0 * (product[2][0] - product[0][2]),
            dipoles[0] * field_dip[1]
            - dipoles[1] * field_dip[0]
            - 2.0 * (product[0][1] - product[1][0]),
        ]
    )
    return (slow_force, torque)


def bonded_energy(coords, selector, bond_length, bond_count, term_count):
    picked_all = jnp.dot(
        coords, selector, precision=lax.Precision.HIGHEST, preferred_element_type=jnp.float32
    )
    second_end = 2 * bond_count
    bond_first = picked_all[:, 0:bond_count]
    bond_second = picked_all[:, bond_count:second_end]
    column_list = [
        picked_all[:, second_end + term_count * j : second_end + term_count * (j + 1)]
        for j in range(7)
    ]
    angle_rows = column_list[0:3]
    torsion_rows = column_list[3:7]
    stretch = bond_second - bond_first
    length_now = jnp.sqrt(jnp.sum(stretch * stretch, 0) + 0.01)
    bond_gap = length_now - bond_length
    bond_part = 0.5 * BOND_K * jnp.sum(bond_gap * bond_gap)
    arm_first = angle_rows[0] - angle_rows[1]
    arm_second = angle_rows[2] - angle_rows[1]
    cosine = jnp.sum(arm_first * arm_second, 0) * lax.rsqrt(
        (jnp.sum(arm_first * arm_first, 0) + 0.01) * (jnp.sum(arm_second * arm_second, 0) + 0.01)
    )
    angle_gap = cosine - ANGLE_REST
    angle_part = 0.5 * ANGLE_K * jnp.sum(angle_gap * angle_gap)
    bond_one = torsion_rows[1] - torsion_rows[0]
    bond_two = torsion_rows[2] - torsion_rows[1]
    bond_three = torsion_rows[3] - torsion_rows[2]
    normal_one = jnp.cross(bond_one, bond_two, axis=0)
    normal_two = jnp.cross(bond_two, bond_three, axis=0)
    dihedral = jnp.sum(normal_one * normal_two, 0) * lax.rsqrt(
        (jnp.sum(normal_one * normal_one, 0) + 0.1) * (jnp.sum(normal_two * normal_two, 0) + 0.1)
    )
    torsion_part = TORSION_K * jnp.sum(1.0 + dihedral)
    return bond_part + angle_part + torsion_part


def body(
    positions,
    velocities,
    charges,
    dipoles,
    quadrupoles,
    damping,
    inverse_mass,
    bonds,
    bond_length,
    angles,
    torsions,
):
    record = jnp.concatenate(
        [positions, charges[None, :], dipoles, quadrupoles, damping[None, :]], 0
    )
    atoms_dev = positions.shape[1]
    n_blk = lax.axis_size("blk")
    n_rep = lax.axis_size("rep")
    n_sub = lax.axis_size("sub")
    blk_index = lax.axis_index("blk")
    rep_index = lax.axis_index("rep")
    sub_index = lax.axis_index("sub")
    team_atoms = atoms_dev * n_rep * n_sub
    targets = lax.all_gather(record, "rep", axis=1, tiled=True)
    column = jnp.arange(targets.shape[1], dtype=jnp.int32)
    target_ids = (
        (blk_index * n_rep + column // atoms_dev) * n_sub + sub_index
    ) * atoms_dev + column % atoms_dev
    moving = lax.all_gather(record, "sub", axis=1, tiled=True)
    own_offset = rep_index * n_sub * atoms_dev
    source_cols = jnp.arange(moving.shape[1], dtype=jnp.int32)

    def contribution(source, team):
        source_ids = team * team_atoms + own_offset + source_cols
        return tile_gradients(targets, source, target_ids, source_ids)

    def forward(buffer):
        return shifted(buffer, "blk", 1)

    summed = contribution(moving, blk_index)

    def one_way(cycle_step, carry):
        ahead, partial_sum = carry
        ahead = forward(ahead)
        partial_sum = partial_sum + contribution(ahead, (blk_index - cycle_step) % n_blk)
        return (ahead, partial_sum)

    ahead, summed = lax.fori_loop(1, n_blk, one_way, (moving, summed))
    partials = lax.psum_scatter(summed, "rep", scatter_dimension=1, tiled=True)
    slow_force, slow_torque = finish(partials, dipoles, quadrupoles)
    domain_size = atoms_dev * n_sub
    bond_count = bonds.shape[1]
    term_count = angles.shape[1]
    all_index = jnp.concatenate(
        [
            bonds[0],
            bonds[1],
            angles[0],
            angles[1],
            angles[2],
            torsions[0],
            torsions[1],
            torsions[2],
            torsions[3],
        ],
        0,
    )
    atom_rows = jnp.arange(domain_size, dtype=jnp.int32)
    selector = (atom_rows[:, None] == all_index[None, :]).astype(jnp.float32)

    def bonded_push(coords):
        domain_coords = lax.all_gather(coords, "sub", axis=1, tiled=True)
        local_push = -jax.grad(bonded_energy)(
            domain_coords, selector, bond_length, bond_count, term_count
        )
        return lax.psum_scatter(local_push, "sub", scatter_dimension=1, tiled=True)

    inner_dt = OUTER_DT / INNER
    velocity = velocities + 0.5 * OUTER_DT * slow_force * inverse_mass[None, :]
    coords = positions
    push = bonded_push(coords)
    for substep in range(INNER):
        velocity = velocity + 0.5 * inner_dt * push * inverse_mass[None, :]
        coords = coords + inner_dt * velocity
        push = bonded_push(coords)
        velocity = velocity + 0.5 * inner_dt * push * inverse_mass[None, :]
    return (coords, velocity, slow_force, slow_torque)


def solution(mesh):
    placed = (
        P(None, ("groups", "blk", "rep", "sub")),
        P(None, ("groups", "blk", "rep", "sub")),
        P(("groups", "blk", "rep", "sub")),
        P(None, ("groups", "blk", "rep", "sub")),
        P(None, ("groups", "blk", "rep", "sub")),
        P(("groups", "blk", "rep", "sub")),
        P(("groups", "blk", "rep", "sub")),
        P(None, ("groups", "blk", "rep", "sub")),
        P(("groups", "blk", "rep", "sub")),
        P(None, ("groups", "blk", "rep", "sub")),
        P(None, ("groups", "blk", "rep", "sub")),
    )
    return jax.shard_map(
        body,
        mesh=mesh,
        in_specs=placed,
        out_specs=(
            P(None, ("groups", "blk", "rep", "sub")),
            P(None, ("groups", "blk", "rep", "sub")),
            P(None, ("groups", "blk", "rep", "sub")),
            P(None, ("groups", "blk", "rep", "sub")),
        ),
        check_vma=False,
    )
```

profile of v0, /device:TPU:0, one launch (start us, length us, event | category | flops | bytes accessed | tf_op | source)
XLA Modules:
  0.0 842.8 jit_solution(14745598933274146437)
XLA Ops:
  18.6 8.3 fusion.335
  35.3 172.3 %while.61 = (s32[]{:T(128)}, f32[3,12,256]{2,1,0:T(8,128)S(1)}, f32[14,768]{1,0:T(8,128)S(1)}, f32[3,14,256]{2,0,1:T(4,128)S(1)}, s32[3,256]{1,0:T(4,128)S(1)}, ...) while((s32[]{:T(128)}, f32[3,12,256]{2,1,0:T(8,128)S(1)}, ...), condition=%wide.region_28.29_spmd.clone, body=%wide.region_0.28_spmd.clone.sunk | while | flops 296708352 | bytes 1247653 | solution.py:104
  82.2 7.0 fusion.559
  133.0 7.0 fusion.559
  183.8 7.0 fusion.559
  207.8 505.9 %while.63 = (s32[]{:T(128)}, f32[14,768]{1,0:T(8,128)S(1)}, f32[12,768]{1,0:T(8,128)S(1)}, f32[14,768]{1,0:T(8,128)S(1)}, s32[]{:T(128)}, /*index=5*/s32[]{:T(12...) while((s32[]{:T(128)}, f32[14,768]{1,0:T(8,128)S(1)}, ...), condition=%wide.region_59.60_spmd.clone, body=%wide.region_29.59_spmd.clone.sunk | while | flops 296730624 | bytes 1970199 | solution.py:226
  234.1 152.6 %while.64 = (s32[]{:T(128)}, f32[3,12,256]{2,1,0:T(8,128)S(1)}, f32[14,768]{1,0:T(8,128)S(1)}, f32[3,14,256]{2,0,1:T(4,128)S(1)}, s32[3,256]{1,0:T(4,128)S(1)}, ...) while((s32[]{:T(128)}, f32[3,12,256]{2,1,0:T(8,128)S(1)}, ...), condition=%wide.region_58.58_spmd, body=%wide.region_30.57_spmd.sunk | while | flops 296707584 | bytes 1244577 | solution.py:104
  247.2 7.0 fusion.582
  261.1 6.9 fusion.580
  298.0 7.0 fusion.582
  311.9 6.9 fusion.580
  348.9 7.0 fusion.582
  362.8 6.9 fusion.580
  392.8 152.6 %while.64 = (s32[]{:T(128)}, f32[3,12,256]{2,1,0:T(8,128)S(1)}, f32[14,768]{1,0:T(8,128)S(1)}, f32[3,14,256]{2,0,1:T(4,128)S(1)}, s32[3,256]{1,0:T(4,128)S(1)}, ...) while((s32[]{:T(128)}, f32[3,12,256]{2,1,0:T(8,128)S(1)}, ...), condition=%wide.region_58.58_spmd, body=%wide.region_30.57_spmd.sunk | while | flops 296707584 | bytes 1244577 | solution.py:104
  405.8 7.0 fusion.582
  419.7 6.9 fusion.580
  456.7 7.0 fusion.582
  470.6 6.9 fusion.580
  507.6 7.0 fusion.582
  551.4 152.6 %while.64 = (s32[]{:T(128)}, f32[3,12,256]{2,1,0:T(8,128)S(1)}, f32[14,768]{1,0:T(8,128)S(1)}, f32[3,14,256]{2,0,1:T(4,128)S(1)}, s32[3,256]{1,0:T(4,128)S(1)}, ...) while((s32[]{:T(128)}, f32[3,12,256]{2,1,0:T(8,128)S(1)}, ...), condition=%wide.region_58.58_spmd, body=%wide.region_30.57_spmd.sunk | while | flops 296707584 | bytes 1244577 | solution.py:104
  564.5 7.0 fusion.582
  615.3 7.0 fusion.582
  666.2 7.0 fusion.582
  715.4 7.3 reduce-scatter.17.cloned.1.call-done
  732.5 8.3 fusion.336
  741.9 7.8 reduce-scatter.21.cloned.1.call-done
  759.5 8.3 fusion.337
  768.9 9.0 %reduce-scatter.23.cloned.1.call-done = f32[384,3]{1,0:T(8,128)} async-done(((f32[768,3]{1,0:T(8,128)}), f32[384,3]{1,0:T(8,128)}) %reduce-scatter.23.cloned.1.call-update) | async-done | bytes 4624
  787.5 8.3 fusion.338
  796.9 9.0 %reduce-scatter.25.cloned.1.call-done = f32[384,3]{1,0:T(8,128)} async-done(((f32[768,3]{1,0:T(8,128)}), f32[384,3]{1,0:T(8,128)}) %reduce-scatter.25.cloned.1.call-update) | async-done | bytes 4624
  815.6 8.3 fusion.339
  825.5 8.5 %reduce-scatter.27.cloned.1.call-done = f32[384,3]{1,0:T(8,128)} async-done(((f32[768,3]{1,0:T(8,128)}), f32[384,3]{1,0:T(8,128)}) %reduce-scatter.27.cloned.1.call-update) | async-done | bytes 4624
  (747 shorter events, 573.3 us)
Async XLA Ops:
  7.2 707.2 %reduce-scatter.19.cloned.1.call-start = ((), (), s32[]{:S(2)}) async-start(), calls=%async_computation.7 | async-start | bytes 589824
  12.0 5.9 copy-start.3
  26.9 1.1 copy-start.9
  26.9 1.1 copy-start.10
  26.9 1.1 copy-start.1
  26.9 1.1 copy-start.2
  26.9 1.1 copy-start.5
  27.9 694.8 %reduce-scatter.17.cloned.1.call-start = ((), (), s32[]{:S(2)}) async-start(), calls=%async_computation.6 | async-start | bytes 73728 | tf_op jit(solution)/shard_map/reduce_scatter | solution.py:227
  207.8 506.6 %copy-start.8 = (f32[384]{0:T(512)S(1)}, f32[384]{0:T(512)}, u32[]{:S(2)}) copy-start(f32[384]{0:T(512)} %param.32) | copy-start | bytes 4612
  207.8 515.0 %copy-start.7 = (f32[3,384]{1,0:T(4,128)S(1)}, f32[3,384]{1,0:T(4,128)}, u32[]{:S(2)}) copy-start(f32[3,384]{1,0:T(4,128)} %param.27) | copy-start | bytes 13828
  227.9 6.3 collective-permute-start
  386.8 5.9 collective-permute-start
  545.5 5.9 collective-permute-start
  713.6 0.6 copy-start
  714.3 35.4 %reduce-scatter.21.cloned.1.call-start = ((), (), s32[]{:S(2)}) async-start(), calls=%async_computation.8 | async-start | bytes 589824
  740.8 1.0 copy-start.4
  741.8 36.2 %reduce-scatter.23.cloned.1.call-start = ((), (), s32[]{:S(2)}) async-start(), calls=%async_computation.9 | async-start | bytes 589824
  768.8 37.1 %reduce-scatter.25.cloned.1.call-start = ((), (), s32[]{:S(2)}) async-start(), calls=%async_computation.10 | async-start | bytes 589824
  796.8 37.2 %reduce-scatter.27.cloned.1.call-start = ((), (), s32[]{:S(2)}) async-start(), calls=%async_computation.11 | async-start | bytes 589824
  807.0 7.9 copy-start.6
Sparse Core Ops, SparseCore 0:
  28.0 10.3 reduce-scatter.18
  714.4 8.2 reduce-scatter.16
  741.9 7.7 reduce-scatter.20
  768.9 8.9 reduce-scatter.22
  796.9 8.9 reduce-scatter.24
  825.0 8.9 reduce-scatter.26
where the time goes:
time: 853 us; the launch traced here: 843 us
  other arithmetic  611 us (72%)
  matrix products  70.9 us (8%)
  waiting for transfers between devices  57.4 us (7%)
  loops' own time  52.3 us (6%)
  blocking collectives  17.3 us (2%)
  local copies, waits for them, and re-layouts  16.1 us (2%)
  between operations  15.8 us (2%)
    reduce_sum x168, other arithmetic, inner3(): return left[0] * right[0] + left[1] * right[1] + left[2] * right[2]  354 us
    reduce_sum x36, other arithmetic, pair_energy(): separation = [source[c][None, :] - target_pos[c][:, None] for c in range(3)]  250 us
    dot_general x10, matrix products, bonded_energy(): jnp.dot(coords, selector, precision=lax.Precision.HIGHEST, preferred_elem...  70.9 us
    unnamed x11, waiting for transfers between devices  34.5 us
    another operation x1, loops' own time, body(): ahead, summed = lax.fori_loop(1, n_blk, one_way, (moving, summed))  29.9 us
    another operation x4, loops' own time, tile_gradients(): summed = lax.map(one_block, (target_blocks, id_blocks))  22.4 us
  transfers between devices with their start and end apart: 9, of which 8 were waited for; matrix products, arithmetic and copies ran while one was open for 72% of the time, Pallas kernels for 0%

commit v1 on v0

v1 whole, which is shorter than its diff:
```python
import functools

import jax
import jax.numpy as jnp
from jax import lax
from jax.experimental import pallas as pl
from jax.experimental.pallas import tpu as pltpu
from jax.sharding import PartitionSpec as P

INNER = 4
MESH = pl.DeviceIdType.MESH
LANES = 128
QUAD_INDEX = ((0, 1, 2), (1, 3, 4), (2, 4, 5))
BOND_K = 0.3
ANGLE_K = 4.0
ANGLE_REST = -0.33
TORSION_K = 2.0
OUTER_DT = 0.2
UNROLL = 3


def dot3(left, right):
    return left[0] * right[0] + left[1] * right[1] + left[2] * right[2]


def matvec(quad, vec):
    return [dot3([quad[QUAD_INDEX[a][b]] for b in range(3)], vec) for a in range(3)]


def my_place():
    n_rep = lax.axis_size("rep")
    n_sub = lax.axis_size("sub")
    return (lax.axis_index("blk") * n_rep + lax.axis_index("rep")) * n_sub + lax.axis_index("sub")


def device_at(place):
    n_rep = lax.axis_size("rep")
    n_sub = lax.axis_size("sub")
    return (
        lax.axis_index("groups"),
        place // (n_rep * n_sub),
        (place // n_sub) % n_rep,
        place % n_sub,
    )


def greet(half, place, count):
    barrier = pltpu.get_barrier_semaphore()

    def one(j, _):
        for other in ((place + j) % count, (place + count - j) % count):
            pl.semaphore_signal(
                barrier, inc=1, device_id=device_at(other), device_id_type=MESH
            )
        return 0

    lax.fori_loop(1, half + 1, one, 0)
    pl.semaphore_wait(barrier, 2 * half)


def gather_kernel(count, own_ref, out_ref, send_sem, recv_sem):
    half = count // 2
    width = own_ref.shape[1]
    place = my_place()
    greet(half, place, count)

    def copy(j):
        return pltpu.make_async_remote_copy(
            src_ref=own_ref,
            dst_ref=out_ref.at[:, pl.ds(pl.multiple_of(j * width, LANES), width)],
            send_sem=send_sem.at[j],
            recv_sem=recv_sem.at[j],
            device_id=device_at((place + count - j) % count),
            device_id_type=MESH,
        )

    def start(j, _):
        copy(j).start()
        return 0

    def finish_one(j, _):
        copy(j).wait()
        return 0

    lax.fori_loop(1, half + 1, start, 0)
    out_ref[:, 0:width] = own_ref[...]
    lax.fori_loop(1, half + 1, finish_one, 0)


def reduce_kernel(count, part_ref, out_ref, land_ref, send_sem, recv_sem):
    half = count // 2
    width = out_ref.shape[1]
    place = my_place()
    greet(half, place, count)

    def copy(j):
        return pltpu.make_async_remote_copy(
            src_ref=part_ref.at[:, pl.ds(pl.multiple_of(j * width, LANES), width)],
            dst_ref=land_ref.at[j],
            send_sem=send_sem.at[j],
            recv_sem=recv_sem.at[j],
            device_id=device_at((place + j) % count),
            device_id_type=MESH,
        )

    def start(j, _):
        copy(j).start()
        return 0

    def finish_one(j, total):
        copy(j).wait()
        return total + land_ref[j]

    lax.fori_loop(1, half + 1, start, 0)
    out_ref[...] = lax.fori_loop(1, half + 1, finish_one, part_ref[:, 0:width])


def pair_terms(target, source, alive):
    c_i, d_i, q_i = target[3], target[4:7], target[7:13]
    c_k, d_k, q_k = source[3], source[4:7], source[7:13]
    r = [source[c] - target[c] for c in range(3)]
    s = dot3(r, r) + target[13] * source[13]
    root = lax.rsqrt(s)
    b1 = alive(root)
    inv = root * root
    b3 = b1 * inv
    b5 = b3 * (3.0 * inv)
    b7 = b5 * (5.0 * inv)
    b9 = b7 * (7.0 * inv)
    b11 = b9 * (9.0 * inv)
    f5 = 2.0 * b5
    f7 = 4.0 * b7
    f10 = 4.0 * b5
    w = matvec(q_k, r)
    u = matvec(q_i, r)
    dk = dot3(d_k, r)
    qk = dot3(w, r)
    di = dot3(d_i, r)
    qi = dot3(u, r)
    a_i = c_k * b3 - dk * b5 + qk * b7
    b_i = c_k * b5 - dk * b7 + qk * b9
    g_i = c_k * b7 - dk * b9 + qk * b11
    a_k = c_i * b3 + di * b5 + qi * b7
    b_k = c_i * b5 + di * b7 + qi * b9
    h_i = [f5 * d_k[a] - f7 * w[a] for a in range(3)]
    h_k = [f5 * d_i[a] + f7 * u[a] for a in range(3)]
    br_i = [b_i * r[a] for a in range(3)]
    br_k = [b_k * r[a] for a in range(3)]
    v_i = [br_i[a] + h_i[a] for a in range(3)]
    v_k = [br_k[a] - h_k[a] for a in range(3)]
    on_i = matvec(q_i, [v_i[a] + br_i[a] for a in range(3)])
    on_k = matvec(q_k, [v_k[a] + br_k[a] for a in range(3)])
    qm = (q_i[0] * q_k[0] + q_i[3] * q_k[3] + q_i[5] * q_k[5]) + 2.0 * (
        q_i[1] * q_k[1] + q_i[2] * q_k[2] + q_i[4] * q_k[4]
    )
    alpha = (
        c_i * a_i
        + di * b_i
        + qi * g_i
        + 0.5 * (dot3(d_i, h_i) + f7 * (dot3(d_k, u) + qm))
        - (4.0 * b9) * dot3(u, w)
    )
    push = [
        (a_i * d_i[a] - a_k * d_k[a]) + (on_i[a] + on_k[a]) - alpha * r[a] for a in range(3)
    ]

    def quad_rows(v, q):
        return [
            r[0] * v[0] + f5 * q[0],
            (r[0] * v[1] + r[1] * v[0]) + f10 * q[1],
            (r[0] * v[2] + r[2] * v[0]) + f10 * q[2],
            r[1] * v[1] + f5 * q[3],
            (r[1] * v[2] + r[2] * v[1]) + f10 * q[4],
            r[2] * v[2] + f5 * q[5],
        ]

    f_i = [a_i * r[a] + b3 * d_k[a] - f5 * w[a] for a in range(3)]
    f_k = [b3 * d_i[a] + f5 * u[a] - a_k * r[a] for a in range(3)]
    return push, f_i + quad_rows(v_i, q_k), f_k + quad_rows(v_k, q_i)


def pair_kernel(count, own_ref, all_ref, out_ref, acc_ref, tgt_ref):
    half = count // 2
    rows = own_ref.shape[0]
    chunks = rows // LANES
    lower = my_place() < half
    lane = lax.broadcasted_iota(jnp.int32, (8, LANES), 1)
    sublane = lax.broadcasted_iota(jnp.int32, (8, LANES), 0)
    diff = lane - sublane
    acc_ref[...] = jnp.zeros_like(acc_ref)
    zero = jnp.zeros((8, LANES), jnp.float32)

    def source_at(start):
        return [all_ref[c : c + 1, pl.ds(start, LANES)] for c in range(14)]

    def one_group(group, _):
        base = pl.multiple_of(group * 8, 8)
        target = [
            jnp.broadcast_to(own_ref[pl.ds(base, 8), c : c + 1], (8, LANES)) for c in range(14)
        ]

        def near(chunk, sums):
            start = pl.multiple_of(chunk * LANES, LANES)

            def alive(root):
                return jnp.where(diff == base - start, 0.0, root)

            push, on_i, _ = pair_terms(target, source_at(start), alive)
            return tuple(x + y for x, y in zip(sums, push + on_i))

        def far(chunk, sums):
            start = pl.multiple_of(chunk * LANES, LANES)
            push, on_i, on_k = pair_terms(target, source_at(start), lambda root: root)
            for c in range(3):
                acc_ref[8 * c : 8 * c + 8, pl.ds(start, LANES)] -= push[c]
            for c in range(9):
                acc_ref[24 + 8 * c : 32 + 8 * c, pl.ds(start, LANES)] += on_k[c]
            return tuple(x + y for x, y in zip(sums, push + on_i))

        first = lax.rem(base // LANES + jnp.where(lower, 0, 1), 2)

        def last(step, sums):
            return far(half * chunks + first + 2 * step, sums)

        sums = lax.fori_loop(0, chunks, near, (zero,) * 12)
        sums = lax.fori_loop(chunks, half * chunks, far, sums, unroll=UNROLL)
        sums = lax.fori_loop(0, (chunks - first + 1) // 2, last, sums)
        tgt_ref[pl.ds(base, 8), :] = jnp.concatenate(
            [jnp.sum(x, axis=1, keepdims=True) for x in sums]
            + [jnp.zeros((8, LANES - 12), jnp.float32)],
            axis=1,
        )
        return 0

    lax.fori_loop(0, rows // 8, one_group, 0)

    def fold(chunk, _):
        at = pl.ds(pl.multiple_of(chunk * LANES, LANES), LANES)
        out_ref[:, at] = jnp.concatenate(
            [jnp.sum(acc_ref[8 * c : 8 * c + 8, at], axis=0, keepdims=True) for c in range(12)]
            + [jnp.zeros((4, LANES), jnp.float32)],
            axis=0,
        )
        return 0

    lax.fori_loop(chunks, (half + 1) * chunks, fold, 0)
    for c in range(chunks):
        flipped = tgt_ref[c * LANES : (c + 1) * LANES, :].T
        out_ref[:, c * LANES : (c + 1) * LANES] = flipped[0:16]


def finish(sums, dipoles, quadrupoles):
    q = [quadrupoles[c] for c in range(6)]
    d = [dipoles[c] for c in range(3)]
    force = sums[0:3]
    field = [-sums[3 + a] for a in range(3)]
    halves = (1.0, 0.5, 0.5, 1.0, 0.5, 1.0)
    g = [halves[c] * sums[6 + c] for c in range(6)]

    def product(a, b):
        return dot3(
            [q[QUAD_INDEX[a][c]] for c in range(3)], [g[QUAD_INDEX[c][b]] for c in range(3)]
        )

    torque = jnp.stack(
        [
            d[1] * field[2] - d[2] * field[1] - 2.0 * (product(1, 2) - product(2, 1)),
            d[2] * field[0] - d[0] * field[2] - 2.0 * (product(2, 0) - product(0, 2)),
            d[0] * field[1] - d[1] * field[0] - 2.0 * (product(0, 1) - product(1, 0)),
        ]
    )
    return force, torque


def cross3(a, b):
    return [
        a[1] * b[2] - a[2] * b[1],
        a[2] * b[0] - a[0] * b[2],
        a[0] * b[1] - a[1] * b[0],
    ]


def minus(a, b):
    return [x - y for x, y in zip(a, b)]


def bond_push(first, second, rest):
    step = minus(second, first)
    sq = dot3(step, step) + 0.01
    scale = BOND_K * (1.0 - rest * lax.rsqrt(sq))
    pull = [scale * x for x in step]
    return [pull, [-x for x in pull]]


def angle_push(first, centre, third):
    a = minus(first, centre)
    b = minus(third, centre)
    ia = lax.rsqrt(dot3(a, a) + 0.01)
    ib = lax.rsqrt(dot3(b, b) + 0.01)
    cosine = dot3(a, b) * (ia * ib)
    lead = -ANGLE_K * (cosine - ANGLE_REST)
    both = lead * (ia * ib)
    on_a = lead * cosine * (ia * ia)
    on_b = lead * cosine * (ib * ib)
    fa = [both * y - on_a * x for x, y in zip(a, b)]
    fb = [both * x - on_b * y for x, y in zip(a, b)]
    return [fa, [-x - y for x, y in zip(fa, fb)], fb]


def torsion_push(p0, p1, p2, p3):
    one = minus(p1, p0)
    two = minus(p2, p1)
    three = minus(p3, p2)
    m = cross3(one, two)
    n = cross3(two, three)
    im = lax.rsqrt(dot3(m, m) + 0.1)
    in_ = lax.rsqrt(dot3(n, n) + 0.1)
    both = -TORSION_K * (im * in_)
    dih = dot3(m, n) * both
    cm = dih * (im * im)
    cn = dih * (in_ * in_)
    gm = [both * y - cm * x for x, y in zip(m, n)]
    gn = [both * x - cn * y for x, y in zip(m, n)]
    f_one = cross3(two, gm)
    f_three = cross3(gn, two)
    f_two = [x + y for x, y in zip(cross3(gm, one), cross3(three, gn))]
    return [
        [-x for x in f_one],
        minus(f_one, f_two),
        minus(f_two, f_three),
        f_three,
    ]


def split3(x):
    top = x.astype(jnp.bfloat16)
    rest = x - top.astype(jnp.float32)
    mid = rest.astype(jnp.bfloat16)
    low = (rest - mid.astype(jnp.float32)).astype(jnp.bfloat16)
    return jnp.concatenate([top, mid, low], axis=0)


def merge3(x):
    n = x.shape[0] // 3
    return x[0:n] + x[n : 2 * n] + x[2 * n : 3 * n]


def bonded_kernel(high, n_bond, n_term, pos_ref, vel_ref, slow_ref, mass_ref, idx_ref, len_ref, x_out, v_out, lo_ref, hi_ref):
    total = idx_ref.shape[1]
    index = idx_ref[...]
    hi_part = index // LANES
    lo_part = index - hi_part * LANES
    lo_rows = lax.broadcasted_iota(jnp.int32, (LANES, total), 0)
    lo_ref[...] = jnp.where(lo_rows == lo_part, 1.0, 0.0).astype(jnp.bfloat16)
    hi_rows = lax.broadcasted_iota(jnp.int32, (high, total), 0)
    hi_ref[...] = jnp.where(hi_rows == hi_part, 1.0, 0.0)
    mass = jnp.concatenate([mass_ref[...]] * 3, axis=0)
    rest = len_ref[...]

    def push_at(coords):
        looked = merge3(
            jnp.dot(split3(coords), lo_ref[...], preferred_element_type=jnp.float32)
        )
        hi = hi_ref[...]
        row = [
            jnp.sum(looked[c * high : (c + 1) * high] * hi, axis=0, keepdims=True)
            for c in range(3)
        ]
        cuts = [(0, n_bond), (n_bond, 2 * n_bond)]
        cuts += [(2 * n_bond + j * n_term, 2 * n_bond + (j + 1) * n_term) for j in range(7)]
        atoms = [[row[c][:, lo:up] for c in range(3)] for lo, up in cuts]
        pushes = (
            bond_push(atoms[0], atoms[1], rest)
            + angle_push(*atoms[2:5])
            + torsion_push(*atoms[5:9])
        )
        spread = jnp.concatenate(
            [jnp.concatenate([p[c] for p in pushes], axis=1) * hi for c in range(3)], axis=0
        )
        return merge3(
            lax.dot_general(
                split3(spread),
                lo_ref[...],
                (((1,), (1,)), ((), ())),
                preferred_element_type=jnp.float32,
            )
        )

    dt = OUTER_DT / INNER
    x = pos_ref[...]
    v = vel_ref[...] + (0.5 * OUTER_DT) * slow_ref[...] * mass
    half = (0.5 * dt) * mass
    v = v + half * push_at(x)

    def substep(step, carry):
        x, v = carry
        x = x + dt * v
        kick = half * push_at(x)
        v = v + kick
        v = v + jnp.where(step < INNER - 1, kick, 0.0)
        return x, v

    x, v = lax.fori_loop(0, INNER, substep, (x, v))
    x_out[...] = x
    v_out[...] = v


def body(
    positions,
    velocities,
    charges,
    dipoles,
    quadrupoles,
    damping,
    inverse_mass,
    bonds,
    bond_length,
    angles,
    torsions,
):
    atoms = positions.shape[1]
    n_sub = lax.axis_size("sub")
    sub = lax.axis_index("sub")
    record = jnp.concatenate(
        [positions, charges[None, :], dipoles, quadrupoles, damping[None, :]], 0
    )
    padded = jnp.concatenate([record, jnp.zeros((2, atoms), jnp.float32)], 0)
    own = padded.T
    count = lax.axis_size("blk") * lax.axis_size("rep") * n_sub
    half = count // 2
    slots = half + 1
    vmem = pl.BlockSpec(memory_space=pltpu.VMEM)

    def remote(kernel, name, ident, width, scratch):
        return pl.pallas_call(
            functools.partial(kernel, count),
            out_shape=jax.ShapeDtypeStruct((16, width), jnp.float32),
            in_specs=[vmem],
            out_specs=vmem,
            scratch_shapes=scratch
            + [pltpu.SemaphoreType.DMA((slots,)), pltpu.SemaphoreType.DMA((slots,))],
            compiler_params=pltpu.CompilerParams(
                collective_id=ident, vmem_limit_bytes=48 * 1024 * 1024
            ),
            name=name,
        )

    everyone = remote(gather_kernel, "gather", 1, slots * atoms, [])(padded)
    parts = pl.pallas_call(
        functools.partial(pair_kernel, count),
        out_shape=jax.ShapeDtypeStruct((16, slots * atoms), jnp.float32),
        in_specs=[vmem, vmem],
        out_specs=vmem,
        scratch_shapes=[
            pltpu.VMEM((96, slots * atoms), jnp.float32),
            pltpu.VMEM((atoms, LANES), jnp.float32),
        ],
        compiler_params=pltpu.CompilerParams(vmem_limit_bytes=48 * 1024 * 1024),
        name="pairs",
    )(own, everyone)
    sums = remote(
        reduce_kernel, "reduce", 2, atoms, [pltpu.VMEM((slots, 16, atoms), jnp.float32)]
    )(parts)
    slow_force, slow_torque = finish(sums, dipoles, quadrupoles)

    def both(mine):
        return lax.all_gather(mine, "sub", axis=1, tiled=True)

    n_term = angles.shape[1] * n_sub
    n_bond = bonds.shape[1] * n_sub
    shared = both(
        jnp.concatenate(
            [positions, velocities, inverse_mass[None, :], bond_length[None, :]], 0
        )
    )
    bonds_all = both(bonds)
    terms_all = both(jnp.concatenate([angles, torsions], 0))
    index = jnp.concatenate([bonds_all.reshape(-1), terms_all.reshape(-1)])[None, :]
    slow_all = both(slow_force)
    size = atoms * n_sub
    used = size // LANES
    high = -(-used // 8) * 8

    def tiled(rows):
        count = rows.shape[0]
        cut = rows.reshape(count, used, LANES)
        return jnp.pad(cut, ((0, 0), (0, high - used), (0, 0))).reshape(count * high, LANES)

    total = index.shape[1]

    def kernel(*refs):
        bonded_kernel(high, n_bond, n_term, *refs)

    state = jax.ShapeDtypeStruct((3 * high, LANES), jnp.float32)
    x_new, v_new = pl.pallas_call(
        kernel,
        out_shape=(state, state),
        in_specs=[vmem] * 6,
        out_specs=(vmem, vmem),
        scratch_shapes=[
            pltpu.VMEM((LANES, total), jnp.bfloat16),
            pltpu.VMEM((high, total), jnp.float32),
        ],
        compiler_params=pltpu.CompilerParams(vmem_limit_bytes=48 * 1024 * 1024),
        name="bonded",
    )(
        tiled(shared[0:3]),
        tiled(shared[3:6]),
        tiled(slow_all),
        tiled(shared[6:7]),
        index,
        shared[7:8],
    )

    def mine(state):
        flat = state.reshape(3, high * LANES)
        return lax.dynamic_slice_in_dim(flat, sub * atoms, atoms, axis=1)

    return (mine(x_new), mine(v_new), slow_force, slow_torque)


def solution(mesh):
    placed = (
        P(None, ("groups", "blk", "rep", "sub")),
        P(None, ("groups", "blk", "rep", "sub")),
        P(("groups", "blk", "rep", "sub")),
        P(None, ("groups", "blk", "rep", "sub")),
        P(None, ("groups", "blk", "rep", "sub")),
        P(("groups", "blk", "rep", "sub")),
        P(("groups", "blk", "rep", "sub")),
        P(None, ("groups", "blk", "rep", "sub")),
        P(("groups", "blk", "rep", "sub")),
        P(None, ("groups", "blk", "rep", "sub")),
        P(None, ("groups", "blk", "rep", "sub")),
    )
    return jax.shard_map(
        body,
        mesh=mesh,
        in_specs=placed,
        out_specs=(
            P(None, ("groups", "blk", "rep", "sub")),
            P(None, ("groups", "blk", "rep", "sub")),
            P(None, ("groups", "blk", "rep", "sub")),
            P(None, ("groups", "blk", "rep", "sub")),
        ),
        check_vma=False,
    )
```

time: 853 us -> 123 us (0.14); the launches traced: 843 us -> 122 us
  other arithmetic: 611 us -> 0.71 us
  Pallas kernels: 0 us -> 107 us
  matrix products: 70.9 us -> 0 us
  waiting for transfers between devices: 57.4 us -> 0 us
  loops' own time: 52.3 us -> 0 us
  between operations: 15.8 us -> 0.83 us
  blocking collectives: 17.3 us -> 7.25 us
  local copies, waits for them, and re-layouts: 16.1 us -> 6.48 us
    reduce_sum x219 -> x0, other arithmetic: 605 us -> none  [the longest x168 354 us: inner3(): return left[0] * right[0] + left[1] * right[1] + left[2] * right[2]]
    pallas_call x0 -> x4, Pallas kernels: none -> 107 us  [the longest x1 71.3 us: body(): pl.pallas_call(functools.partial(pair_kernel, count), out_shape=jax.Shape...]
    dot_general x10 -> x0, matrix products: 70.9 us -> none  [bonded_energy(): jnp.dot(coords, selector, precision=lax.Precision.HIGHEST, preferred_elem...]
    another operation x5 -> x0, loops' own time: 52.3 us -> none  [the longest x1 29.9 us: body(): ahead, summed = lax.fori_loop(1, n_blk, one_way, (moving, summed))]
    unnamed x11 -> x0, waiting for transfers between devices: 34.5 us -> none
    ppermute x3 -> x0, waiting for transfers between devices: 15.6 us -> none  [shifted(): lax.ppermute(array, axis, [(i, (i + by) % count) for i in range(count)])]
    all_gather x7 -> x4, blocking collectives: 17.3 us -> 7.25 us  [both(): return lax.all_gather(mine, 'sub', axis=1, tiled=True)]
  transfers between devices with their start and end apart: 9 -> 0, of which waited for: 8 -> 0; matrix products, arithmetic and copies ran while one was open for 72% -> 0% of each run, Pallas kernels for 0% -> 0%
where the time goes in v1:
time: 123 us; the launch traced here: 122 us
  Pallas kernels  107 us (87%)
  blocking collectives  7.25 us (6%)
  local copies, waits for them, and re-layouts  6.48 us (5%)
    pallas_call x1, Pallas kernels, body(): pl.pallas_call(functools.partial(pair_kernel, count), out_shape=jax.Shape...  71.3 us
    pallas_call x1, Pallas kernels, body(): everyone = remote(gather_kernel, 'gather', 1, slots * atoms, [])(padded)  13.7 us
    pallas_call x1, Pallas kernels, body(): pl.pallas_call(kernel, out_shape=(state, state), in_specs=[vmem] * 6, out...  11.2 us
    pallas_call x1, Pallas kernels, body(): remote(reduce_kernel, 'reduce', 2, atoms, [pltpu.VMEM((slots, 16, atoms),...  10.3 us
    all_gather x4, blocking collectives, both(): return lax.all_gather(mine, 'sub', axis=1, tiled=True)  7.25 us
    unnamed x22, local copies, waits for them, and re-layouts  2.81 us

profile of v1, /device:TPU:0, one launch (start us, length us, event | category | flops | bytes accessed | tf_op | source)
XLA Modules:
  0.0 121.8 jit_solution(4535313249760752364)
XLA Ops:
  0.6 0.0 copy-start.8
  0.6 0.0 copy-start.1
  0.7 0.7 broadcast_in_dim.20
  1.3 0.0 copy-done.8
  1.4 0.0 copy-done.1
  1.4 1.5 %concatenate.13.own_ref = f32[16,384]{1,0:T(8,128)S(1)} concatenate(f32[3,384]{1,0:T(4,128)} %param.11, f32[1,384]{1,0:T(1,128)S(1)} %broadcast_in_dim.20, f32[3,384]{1,0:T(4,128)S(1)} %copy-done.1, f32[6,384]{1,0:T(8,128)} %param.15, f32[1,384]{1,0:T(1,128)S(1)} %broadcast_in_dim.21, f32[2,384]{1,0:T(2,128)S(1)} %broadcast_in_dim.22), dimensions={0} | concatenate | bytes 49152 | tf_op jit(solution)/shard_map/concatenate | solution.py:427
  2.9 13.7 %gather.1.all_ref = f32[16,3456]{1,0:T(8,128)S(1)} custom-call(f32[16,384]{1,0:T(8,128)S(1)} %concatenate.13.own_ref), custom_call_target="tpu_custom_call" | custom-call | tf_op jit(solution)/shard_map/gather/pallas_call | solution.py:448
  16.7 0.1 copy.25
  16.8 71.3 %pairs.1.part_ref = f32[16,3456]{1,0:T(8,128)S(1)} custom-call(f32[384,16]{1,0:T(8,128)S(1)} %bitcast.11, f32[16,3456]{1,0:T(8,128)S(1)} %gather.1.all_ref), custom_call_target="tpu_custom_call" | custom-call | tf_op jit(solution)/shard_map/pairs/pallas_call | solution.py:449
  88.1 10.3 %reduce.3 = f32[16,384]{1,0:T(8,128)S(1)} custom-call(f32[16,3456]{1,0:T(8,128)S(1)} %pairs.1.part_ref), custom_call_target="tpu_custom_call" | custom-call | tf_op jit(solution)/shard_map/reduce/pallas_call | solution.py:461
  98.4 0.0 copy-start.3
  98.4 1.8 %all_gather.13 = f32[3,768]{1,0:T(4,128)S(1)} all-gather(f32[3,384]{1,0:T(4,128)S(1)} %slice.94), channel_id=1, replica_groups=mesh['groups'=2,'blk'=4,'rep'=2,'sub'=2] {'sub'}, dimensions={1}, use_global_device_ids=true | all-gather | bytes 13824 | tf_op jit(solution)/shard_map/all_gather | solution.py:467
  100.2 0.0 copy-start.9
  100.2 0.0 copy-start.10
  100.2 0.0 copy-start.6
  100.2 0.6 copy-done.9
  100.9 0.0 copy-done.10
  100.9 0.0 copy-done.6
  100.9 0.7 copy-done.2
  101.6 1.8 %all_gather.12 = f32[8,768]{1,0:T(8,128)S(1)} all-gather(f32[8,384]{1,0:T(8,128)S(1)} %pad_maximum_fusion), channel_id=1, replica_groups=mesh['groups'=2,'blk'=4,'rep'=2,'sub'=2] {'sub'}, dimensions={1}, use_global_device_ids=true | all-gather | bytes 36864 | tf_op jit(solution)/shard_map/all_gather | solution.py:467
  103.5 0.0 copy-start.4
  103.5 0.0 copy-start.5
  103.5 0.7 copy-done.4
  104.2 0.0 copy-done.5
  104.2 1.8 %all_gather.15 = s32[7,1536]{1,0:T(8,128)S(1)} all-gather(s32[7,768]{1,0:T(8,128)S(1)} %pad_add_fusion.1), channel_id=1, replica_groups=mesh['groups'=2,'blk'=4,'rep'=2,'sub'=2] {'sub'}, dimensions={1}, use_global_device_ids=true | all-gather | bytes 64512 | tf_op jit(solution)/shard_map/all_gather | solution.py:467
  106.0 0.7 copy-done.7
  106.7 1.8 %all_gather.14 = s32[2,768]{1,0:T(2,128)S(1)} all-gather(s32[2,384]{1,0:T(2,128)S(1)} %copy-done.7), channel_id=1, replica_groups=mesh['groups'=2,'blk'=4,'rep'=2,'sub'=2] {'sub'}, dimensions={1}, use_global_device_ids=true | all-gather | bytes 9216 | tf_op jit(solution)/shard_map/all_gather | solution.py:467
  108.5 11.2 %bonded.1 = (f32[24,128]{1,0:T(8,128)S(1)}, f32[24,128]{1,0:T(8,128)S(1)}) custom-call(f32[24,128]{1,0:T(8,128)S(1)} %get-tuple-element.13.refs_0_, f32[24,128]{1,0:T(8,128)S(1)} %get-tuple-element.12.refs_1_, f32[24,128]{1,0:T(8,128)S(1)} %pad_bitcast_fusion.refs_2_, f32[8,128]{1,0:T(8,128)S(1)} %pad_bitcast_fusion.3.refs_3_, s32[1,12288]{1,0:T(1,128)S(1)} %bitcast.12, ...), custom_call_target="tpu_custom_call" | custom-call | tf_op jit(solution)/shard_map/bonded/pallas_call | solution.py:495
  119.8 0.6 constant_dynamic-slice_fusion
  120.4 0.6 constant_dynamic-slice_fusion.1
  121.0 0.1 copy-done
  121.2 0.6 pad_maximum_fusion.1
  (27 shorter events, 0.2 us)
Async XLA Ops:
  0.6 0.7 copy-start.8
  0.6 0.7 copy-start.1
  98.4 1.8 %copy-start.3 = (f32[3,384]{1,0:T(4,128)}, f32[3,384]{1,0:T(4,128)S(1)}, u32[]{:S(2)}) copy-start(f32[3,384]{1,0:T(4,128)S(1)} %slice.94) | copy-start | bytes 13828
  100.2 0.7 copy-start.9
  100.2 0.7 copy-start.10
  100.2 0.7 copy-start.6
  100.9 0.7 copy-start.2
  103.5 0.7 copy-start.4
  103.5 0.7 copy-start.5
  106.0 0.7 copy-start.7
  120.4 0.7 copy-start

commit v2 on v1

--- a/solution.py
+++ b/solution.py
@@ -58,10 +58,13 @@
     pl.semaphore_wait(barrier, 2 * half)
 
 
-def gather_kernel(count, own_ref, out_ref, send_sem, recv_sem):
+def gather_kernel(
+    count, own_ref, pack_ref, out_ref, both_ref, send_sem, recv_sem, pack_send, pack_recv
+):
     half = count // 2
     width = own_ref.shape[1]
     place = my_place()
+    sub = lax.axis_index("sub")
     greet(half, place, count)
 
     def copy(j):
@@ -83,36 +86,19 @@
         return 0
 
     lax.fori_loop(1, half + 1, start, 0)
+    swap = pltpu.make_async_remote_copy(
+        src_ref=pack_ref,
+        dst_ref=both_ref.at[sub],
+        send_sem=pack_send,
+        recv_sem=pack_recv,
+        device_id=device_at(place + 1 - 2 * sub),
+        device_id_type=MESH,
+    )
+    swap.start()
     out_ref[:, 0:width] = own_ref[...]
+    both_ref[sub] = pack_ref[...]
+    swap.wait()
     lax.fori_loop(1, half + 1, finish_one, 0)
-
-
-def reduce_kernel(count, part_ref, out_ref, land_ref, send_sem, recv_sem):
-    half = count // 2
-    width = out_ref.shape[1]
-    place = my_place()
-    greet(half, place, count)
-
-    def copy(j):
-        return pltpu.make_async_remote_copy(
-            src_ref=part_ref.at[:, pl.ds(pl.multiple_of(j * width, LANES), width)],
-            dst_ref=land_ref.at[j],
-            send_sem=send_sem.at[j],
-            recv_sem=recv_sem.at[j],
-            device_id=device_at((place + j) % count),
-            device_id_type=MESH,
-        )
-
-    def start(j, _):
-        copy(j).start()
-        return 0
-
-    def finish_one(j, total):
-        copy(j).wait()
-        return total + land_ref[j]
-
-    lax.fori_loop(1, half + 1, start, 0)
-    out_ref[...] = lax.fori_loop(1, half + 1, finish_one, part_ref[:, 0:width])
 
 
 def pair_terms(target, source, alive):
@@ -249,10 +235,7 @@
         out_ref[:, c * LANES : (c + 1) * LANES] = flipped[0:16]
 
 
-def finish(sums, dipoles, quadrupoles):
-    q = [quadrupoles[c] for c in range(6)]
-    d = [dipoles[c] for c in range(3)]
-    force = sums[0:3]
+def torque_of(sums, d, q):
     field = [-sums[3 + a] for a in range(3)]
     halves = (1.0, 0.5, 0.5, 1.0, 0.5, 1.0)
     g = [halves[c] * sums[6 + c] for c in range(6)]
@@ -262,14 +245,14 @@
             [q[QUAD_INDEX[a][c]] for c in range(3)], [g[QUAD_INDEX[c][b]] for c in range(3)]
         )
 
-    torque = jnp.stack(
+    return jnp.concatenate(
         [
             d[1] * field[2] - d[2] * field[1] - 2.0 * (product(1, 2) - product(2, 1)),
             d[2] * field[0] - d[0] * field[2] - 2.0 * (product(2, 0) - product(0, 2)),
             d[0] * field[1] - d[1] * field[0] - 2.0 * (product(0, 1) - product(1, 0)),
-        ]
-    )
-    return force, torque
+        ],
+        axis=0,
+    )
 
 
 def cross3(a, b):
@@ -345,17 +328,87 @@
     return x[0:n] + x[n : 2 * n] + x[2 * n : 3 * n]
 
 
-def bonded_kernel(high, n_bond, n_term, pos_ref, vel_ref, slow_ref, mass_ref, idx_ref, len_ref, x_out, v_out, lo_ref, hi_ref):
-    total = idx_ref.shape[1]
-    index = idx_ref[...]
+def final_kernel(
+    count,
+    high,
+    part_ref,
+    both_ref,
+    dip_ref,
+    quad_ref,
+    x_out,
+    v_out,
+    f_out,
+    t_out,
+    land_ref,
+    force_ref,
+    lo_ref,
+    hi_ref,
+    send_sem,
+    recv_sem,
+    force_send,
+    force_recv,
+):
+    half = count // 2
+    width = f_out.shape[1]
+    chunks = width // LANES
+    used = 2 * chunks
+    place = my_place()
+    sub = lax.axis_index("sub")
+    greet(half, place, count)
+
+    def copy(j):
+        return pltpu.make_async_remote_copy(
+            src_ref=part_ref.at[:, pl.ds(pl.multiple_of(j * width, LANES), width)],
+            dst_ref=land_ref.at[j],
+            send_sem=send_sem.at[j],
+            recv_sem=recv_sem.at[j],
+            device_id=device_at((place + j) % count),
+            device_id_type=MESH,
+        )
+
+    def start(j, _):
+        copy(j).start()
+        return 0
+
+    def finish_one(j, total):
+        copy(j).wait()
+        return total + land_ref[j]
+
+    lax.fori_loop(1, half + 1, start, 0)
+
+    rows = both_ref.shape[1]
+    n_mult = (rows - 10) // 7
+    n_bond = 2 * width
+    n_term = n_mult * n_bond
+    total_terms = 2 * n_bond + 7 * n_term
+    index = jnp.concatenate(
+        [both_ref[k, row : row + 1, :] for row in range(8, rows) for k in range(2)], axis=1
+    ).astype(jnp.int32)
     hi_part = index // LANES
     lo_part = index - hi_part * LANES
-    lo_rows = lax.broadcasted_iota(jnp.int32, (LANES, total), 0)
+    lo_rows = lax.broadcasted_iota(jnp.int32, (LANES, total_terms), 0)
     lo_ref[...] = jnp.where(lo_rows == lo_part, 1.0, 0.0).astype(jnp.bfloat16)
-    hi_rows = lax.broadcasted_iota(jnp.int32, (high, total), 0)
+    hi_rows = lax.broadcasted_iota(jnp.int32, (high, total_terms), 0)
     hi_ref[...] = jnp.where(hi_rows == hi_part, 1.0, 0.0)
-    mass = jnp.concatenate([mass_ref[...]] * 3, axis=0)
-    rest = len_ref[...]
+    rest = jnp.concatenate([both_ref[k, 7:8, :] for k in range(2)], axis=1)
+    fill = [jnp.zeros((high - used, LANES), jnp.float32)] if high > used else []
+
+    def tiled(read, wanted):
+        pieces = []
+        for row in wanted:
+            for k in range(2):
+                for c in range(chunks):
+                    pieces.append(read(k, row, c * LANES))
+            pieces += fill
+        return jnp.concatenate(pieces, axis=0)
+
+    def from_pack(k, row, at):
+        return both_ref[k, row : row + 1, at : at + LANES]
+
+    def from_force(k, row, at):
+        return force_ref[k, row : row + 1, at : at + LANES]
+
+    mass = tiled(from_pack, (6, 6, 6))
 
     def push_at(coords):
         looked = merge3(
@@ -387,22 +440,58 @@
         )
 
     dt = OUTER_DT / INNER
-    x = pos_ref[...]
-    v = vel_ref[...] + (0.5 * OUTER_DT) * slow_ref[...] * mass
-    half = (0.5 * dt) * mass
-    v = v + half * push_at(x)
+    x = tiled(from_pack, (0, 1, 2))
+    half_step = (0.5 * dt) * mass
+    v = tiled(from_pack, (3, 4, 5)) + half_step * push_at(x)
+
+    total = lax.fori_loop(1, half + 1, finish_one, part_ref[:, 0:width])
+    force_ref[sub] = total
+    f_out[...] = total[0:3]
+    swap = pltpu.make_async_remote_copy(
+        src_ref=force_ref.at[sub],
+        dst_ref=force_ref.at[sub],
+        send_sem=force_send,
+        recv_sem=force_recv,
+        device_id=device_at(place + 1 - 2 * sub),
+        device_id_type=MESH,
+    )
+    swap.start()
+    t_out[...] = torque_of(
+        [total[c : c + 1] for c in range(12)],
+        [dip_ref[c : c + 1, :] for c in range(3)],
+        [quad_ref[c : c + 1, :] for c in range(6)],
+    )
+    swap.wait()
+    v = v + (0.5 * OUTER_DT) * tiled(from_force, (0, 1, 2)) * mass
 
     def substep(step, carry):
         x, v = carry
         x = x + dt * v
-        kick = half * push_at(x)
+        kick = half_step * push_at(x)
         v = v + kick
         v = v + jnp.where(step < INNER - 1, kick, 0.0)
         return x, v
 
     x, v = lax.fori_loop(0, INNER, substep, (x, v))
-    x_out[...] = x
-    v_out[...] = v
+
+    def mine(state):
+        rows = []
+        for c in range(3):
+            sides = [
+                jnp.concatenate(
+                    [
+                        state[c * high + k * chunks + h : c * high + k * chunks + h + 1]
+                        for h in range(chunks)
+                    ],
+                    axis=1,
+                )
+                for k in range(2)
+            ]
+            rows.append(jnp.where(sub == 0, sides[0], sides[1]))
+        return jnp.concatenate(rows, axis=0)
+
+    x_out[...] = mine(x)
+    v_out[...] = mine(v)
 
 
 def body(
@@ -420,103 +509,76 @@
 ):
     atoms = positions.shape[1]
     n_sub = lax.axis_size("sub")
-    sub = lax.axis_index("sub")
     record = jnp.concatenate(
         [positions, charges[None, :], dipoles, quadrupoles, damping[None, :]], 0
     )
     padded = jnp.concatenate([record, jnp.zeros((2, atoms), jnp.float32)], 0)
     own = padded.T
     count = lax.axis_size("blk") * lax.axis_size("rep") * n_sub
-    half = count // 2
-    slots = half + 1
+    slots = count // 2 + 1
     vmem = pl.BlockSpec(memory_space=pltpu.VMEM)
-
-    def remote(kernel, name, ident, width, scratch):
-        return pl.pallas_call(
-            functools.partial(kernel, count),
-            out_shape=jax.ShapeDtypeStruct((16, width), jnp.float32),
-            in_specs=[vmem],
-            out_specs=vmem,
-            scratch_shapes=scratch
-            + [pltpu.SemaphoreType.DMA((slots,)), pltpu.SemaphoreType.DMA((slots,))],
-            compiler_params=pltpu.CompilerParams(
-                collective_id=ident, vmem_limit_bytes=48 * 1024 * 1024
-            ),
-            name=name,
-        )
-
-    everyone = remote(gather_kernel, "gather", 1, slots * atoms, [])(padded)
+    dma = pltpu.SemaphoreType.DMA
+    indices = jnp.concatenate(
+        [bonds, angles.reshape(-1, atoms), torsions.reshape(-1, atoms)], 0
+    )
+    pack = jnp.concatenate(
+        [
+            positions,
+            velocities,
+            inverse_mass[None, :],
+            bond_length[None, :],
+            indices.astype(jnp.float32),
+        ],
+        0,
+    )
+
+    def params(**more):
+        return pltpu.CompilerParams(vmem_limit_bytes=48 * 1024 * 1024, **more)
+
+    def shape(*dims):
+        return jax.ShapeDtypeStruct(dims, jnp.float32)
+
+    everyone, both = pl.pallas_call(
+        functools.partial(gather_kernel, count),
+        out_shape=(shape(16, slots * atoms), shape(2, *pack.shape)),
+        in_specs=[vmem] * 2,
+        out_specs=(vmem, vmem),
+        scratch_shapes=[dma((slots,)), dma((slots,)), dma, dma],
+        compiler_params=params(collective_id=1),
+        name="gather",
+    )(padded, pack)
     parts = pl.pallas_call(
         functools.partial(pair_kernel, count),
-        out_shape=jax.ShapeDtypeStruct((16, slots * atoms), jnp.float32),
+        out_shape=shape(16, slots * atoms),
         in_specs=[vmem, vmem],
         out_specs=vmem,
         scratch_shapes=[
             pltpu.VMEM((96, slots * atoms), jnp.float32),
             pltpu.VMEM((atoms, LANES), jnp.float32),
         ],
-        compiler_params=pltpu.CompilerParams(vmem_limit_bytes=48 * 1024 * 1024),
+        compiler_params=params(),
         name="pairs",
     )(own, everyone)
-    sums = remote(
-        reduce_kernel, "reduce", 2, atoms, [pltpu.VMEM((slots, 16, atoms), jnp.float32)]
-    )(parts)
-    slow_force, slow_torque = finish(sums, dipoles, quadrupoles)
-
-    def both(mine):
-        return lax.all_gather(mine, "sub", axis=1, tiled=True)
-
-    n_term = angles.shape[1] * n_sub
-    n_bond = bonds.shape[1] * n_sub
-    shared = both(
-        jnp.concatenate(
-            [positions, velocities, inverse_mass[None, :], bond_length[None, :]], 0
-        )
-    )
-    bonds_all = both(bonds)
-    terms_all = both(jnp.concatenate([angles, torsions], 0))
-    index = jnp.concatenate([bonds_all.reshape(-1), terms_all.reshape(-1)])[None, :]
-    slow_all = both(slow_force)
-    size = atoms * n_sub
-    used = size // LANES
-    high = -(-used // 8) * 8
-
-    def tiled(rows):
-        count = rows.shape[0]
-        cut = rows.reshape(count, used, LANES)
-        return jnp.pad(cut, ((0, 0), (0, high - used), (0, 0))).reshape(count * high, LANES)
-
-    total = index.shape[1]
-
-    def kernel(*refs):
-        bonded_kernel(high, n_bond, n_term, *refs)
-
-    state = jax.ShapeDtypeStruct((3 * high, LANES), jnp.float32)
-    x_new, v_new = pl.pallas_call(
-        kernel,
-        out_shape=(state, state),
-        in_specs=[vmem] * 6,
-        out_specs=(vmem, vmem),
+    high = -(-(n_sub * atoms // LANES) // 8) * 8
+    total = n_sub * indices.shape[0] * atoms
+    return pl.pallas_call(
+        functools.partial(final_kernel, count, high),
+        out_shape=(shape(3, atoms),) * 4,
+        in_specs=[vmem] * 4,
+        out_specs=(vmem,) * 4,
         scratch_shapes=[
+            pltpu.VMEM((slots, 16, atoms), jnp.float32),
+            pltpu.VMEM((2, 16, atoms), jnp.float32),
             pltpu.VMEM((LANES, total), jnp.bfloat16),
             pltpu.VMEM((high, total), jnp.float32),
+            dma((slots,)),
+            dma((slots,)),
+            dma,
+            dma,
         ],
-        compiler_params=pltpu.CompilerParams(vmem_limit_bytes=48 * 1024 * 1024),
-        name="bonded",
-    )(
-        tiled(shared[0:3]),
-        tiled(shared[3:6]),
-        tiled(slow_all),
-        tiled(shared[6:7]),
-        index,
-        shared[7:8],
-    )
-
-    def mine(state):
-        flat = state.reshape(3, high * LANES)
-        return lax.dynamic_slice_in_dim(flat, sub * atoms, atoms, axis=1)
-
-    return (mine(x_new), mine(v_new), slow_force, slow_torque)
+        compiler_params=params(collective_id=2),
+        name="finale",
+    )(parts, both, dipoles, quadrupoles)
 
 
 def solution(mesh):

time: 123 us -> 114 us (0.927)
  blocking collectives: 7.25 us -> 0 us
  Pallas kernels: 107 us -> 104 us
  local copies, waits for them, and re-layouts: 6.48 us -> 8.16 us
    all_gather x4 -> x0, blocking collectives: 7.25 us -> none  [both(): return lax.all_gather(mine, 'sub', axis=1, tiled=True)]
    unnamed x22 -> x18, local copies, waits for them, and re-layouts: 2.81 us -> 5.12 us
    pallas_call x4 -> x3, Pallas kernels: 107 us -> 104 us  [the longest x1 71.3 us: body(): pl.pallas_call(functools.partial(pair_kernel, count), out_shape=shape(16,...]
    concatenate x2, local copies, waits for them, and re-layouts: 1.66 us -> 0.26 us  [body(): padded = jnp.concatenate([record, jnp.zeros((2, atoms), jnp.float32)], 0)]
where the time goes in v2:
time: 114 us; the launch traced here: 113 us
  Pallas kernels  104 us (91%)
  local copies, waits for them, and re-layouts  8.16 us (7%)
    pallas_call x1, Pallas kernels, body(): pl.pallas_call(functools.partial(pair_kernel, count), out_shape=shape(16,...  71.3 us
    pallas_call x1, Pallas kernels, body(): pl.pallas_call(functools.partial(final_kernel, count, high), out_shape=(s...  19.3 us
    pallas_call x1, Pallas kernels, body(): pl.pallas_call(functools.partial(gather_kernel, count), out_shape=(shape(...  13.8 us
    unnamed x18, local copies, waits for them, and re-layouts  5.12 us

profile of v2, /device:TPU:0, one launch (start us, length us, event | category | flops | bytes accessed | tf_op | source)
XLA Modules:
  0.0 113.3 jit_solution(8040349376142406784)
XLA Ops:
  0.6 0.0 copy-start.3
  0.6 0.7 broadcast_in_dim.15
  1.3 0.7 broadcast_in_dim.16
  2.0 0.7 broadcast_in_dim.18
  2.7 0.7 broadcast_in_dim.19
  3.4 0.0 copy-done.3
  3.4 0.0 copy-start.4
  3.4 0.7 copy-done.4
  4.1 0.0 copy-start.6
  4.1 0.7 copy-done.6
  4.8 0.0 copy-start.2
  4.8 0.0 copy-start.5
  4.8 0.7 copy-done.2
  5.5 0.0 copy-done.5
  5.5 0.0 copy-start
  5.5 0.0 copy-start.1
  5.5 0.7 copy-done
  6.2 0.0 copy-done.1
  6.2 0.1 concatenate.9.own_ref
  6.3 0.1 copy.25
  6.5 13.8 %gather.1 = (f32[16,3456]{1,0:T(8,128)S(1)}, f32[2,24,384]{2,1,0:T(8,128)S(1)}) custom-call(f32[16,384]{1,0:T(8,128)S(1)} %concatenate.9.own_ref, f32[24,384]{1,0:T(8,128)S(1)} %concatenate.11.pack_ref), custom_call_target="tpu_custom_call" | custom-call | tf_op jit(solution)/shard_map/gather/pallas_call | solution.py:541
  20.2 71.3 %pairs.1.part_ref = f32[16,3456]{1,0:T(8,128)S(1)} custom-call(f32[384,16]{1,0:T(8,128)S(1)} %bitcast.1, f32[16,3456]{1,0:T(8,128)S(1)} %get-tuple-element.6.all_ref), custom_call_target="tpu_custom_call" | custom-call | tf_op jit(solution)/shard_map/pairs/pallas_call | solution.py:550
  91.6 19.3 %finale.1 = (f32[3,384]{1,0:T(4,128)S(1)}, f32[3,384]{1,0:T(4,128)S(1)}, f32[3,384]{1,0:T(4,128)S(1)}, f32[3,384]{1,0:T(4,128)S(1)}) custom-call(f32[16,3456]{1,0:T(8,128)S(1)} %pairs.1.part_ref, f32[2,24,384]{2,1,0:T(8,128)S(1)} %get-tuple-element.7.both_ref, f32[3,384]{1,0:T(4,128)S(1)} %copy-done.1, f32[6,384]{1,0:T(8,128)S(1)} %copy-done), custom_call_target="tpu_custom_call" | custom-call | tf_op jit(solution)/shard_map/finale/pallas_call | solution.py:564
  110.9 0.6 copy.30
  111.5 0.6 copy.31
  112.1 0.6 copy.32
  112.7 0.6 copy.33
  (5 shorter events, 0.1 us)
Async XLA Ops:
  0.6 2.8 %copy-start.3 = (s32[3,768]{1,0:T(4,128)S(1)}, s32[3,768]{1,0:T(4,128)}, u32[]{:S(2)}) copy-start(s32[3,768]{1,0:T(4,128)} %param.20) | copy-start | bytes 27652
  3.4 0.7 copy-start.4
  4.1 0.7 copy-start.6
  4.8 0.7 copy-start.2
  4.8 0.7 copy-start.5
  5.5 0.7 copy-start
  5.5 0.7 copy-start.1

commit v3 on v2

--- a/solution.py
+++ b/solution.py
@@ -59,17 +59,73 @@
 
 
 def gather_kernel(
-    count, own_ref, pack_ref, out_ref, both_ref, send_sem, recv_sem, pack_send, pack_recv
+    count,
+    pos_any,
+    vel_any,
+    dip_any,
+    quad_any,
+    scal_ref,
+    bond_any,
+    angle_any,
+    torsion_any,
+    out_ref,
+    both_ref,
+    own_ref,
+    near_ref,
+    pos_ref,
+    vel_ref,
+    dip_ref,
+    quad_ref,
+    bond_ref,
+    angle_ref,
+    torsion_ref,
+    record_ref,
+    pack_ref,
+    local_sem,
+    send_sem,
+    recv_sem,
+    pack_send,
+    pack_recv,
 ):
     half = count // 2
-    width = own_ref.shape[1]
+    width = pos_any.shape[1]
     place = my_place()
     sub = lax.axis_index("sub")
+    loads = [
+        pltpu.make_async_copy(src, dst, local_sem.at[n])
+        for n, (src, dst) in enumerate(
+            (
+                (pos_any, pos_ref),
+                (vel_any, vel_ref),
+                (dip_any, dip_ref),
+                (quad_any, quad_ref),
+                (bond_any, bond_ref),
+                (angle_any, angle_ref),
+                (torsion_any, torsion_ref),
+            )
+        )
+    ]
+    for load in loads:
+        load.start()
     greet(half, place, count)
+    for load in loads:
+        load.wait()
+
+    record_ref[...] = jnp.concatenate(
+        [
+            pos_ref[...],
+            scal_ref[0:1, :],
+            dip_ref[...],
+            quad_ref[...],
+            scal_ref[1:2, :],
+            jnp.zeros((2, width), jnp.float32),
+        ],
+        axis=0,
+    )
 
     def copy(j):
         return pltpu.make_async_remote_copy(
-            src_ref=own_ref,
+            src_ref=record_ref,
             dst_ref=out_ref.at[:, pl.ds(pl.multiple_of(j * width, LANES), width)],
             send_sem=send_sem.at[j],
             recv_sem=recv_sem.at[j],
@@ -86,6 +142,22 @@
         return 0
 
     lax.fori_loop(1, half + 1, start, 0)
+
+    def cut(ref):
+        whole = ref[...].astype(jnp.float32)
+        return [
+            whole[row : row + 1, at : at + width]
+            for row in range(whole.shape[0])
+            for at in range(0, whole.shape[1], width)
+        ]
+
+    pack_ref[...] = jnp.concatenate(
+        [pos_ref[...], vel_ref[...], scal_ref[2:4, :]]
+        + cut(bond_ref)
+        + cut(angle_ref)
+        + cut(torsion_ref),
+        axis=0,
+    )
     swap = pltpu.make_async_remote_copy(
         src_ref=pack_ref,
         dst_ref=both_ref.at[sub],
@@ -95,10 +167,47 @@
         device_id_type=MESH,
     )
     swap.start()
-    out_ref[:, 0:width] = own_ref[...]
+    out_ref[:, 0:width] = record_ref[...]
     both_ref[sub] = pack_ref[...]
+    wide = jnp.concatenate([record_ref[...], jnp.zeros((LANES - 16, width), jnp.float32)], axis=0)
+    chunks = width // LANES
+    for c in range(chunks):
+        own_ref[c * LANES : (c + 1) * LANES, :] = wide[:, c * LANES : (c + 1) * LANES].T
+    lane = lax.broadcasted_iota(jnp.int32, (8, LANES), 1)
+    sublane = lax.broadcasted_iota(jnp.int32, (8, LANES), 0)
+    diff = lane - sublane
+
+    def one_group(group, _):
+        base = pl.multiple_of(group * 8, 8)
+        target = [
+            jnp.broadcast_to(own_ref[pl.ds(base, 8), c : c + 1], (8, LANES)) for c in range(14)
+        ]
+
+        def near(chunk, sums):
+            at = pl.multiple_of(chunk * LANES, LANES)
+            source = [record_ref[c : c + 1, pl.ds(at, LANES)] for c in range(14)]
+
+            def alive(root):
+                return jnp.where(diff == base - at, 0.0, root)
+
+            push, on_i, _ = pair_terms(target, source, alive)
+            return tuple(x + y for x, y in zip(sums, push + on_i))
+
+        sums = lax.fori_loop(0, chunks, near, (jnp.zeros((8, LANES), jnp.float32),) * 12)
+        near_ref[pl.ds(base, 8), :] = row_sums(sums)
+        return 0
+
+    lax.fori_loop(0, width // 8, one_group, 0)
     swap.wait()
     lax.fori_loop(1, half + 1, finish_one, 0)
+
+
+def row_sums(sums):
+    return jnp.concatenate(
+        [jnp.sum(x, axis=1, keepdims=True) for x in sums]
+        + [jnp.zeros((8, LANES - len(sums)), jnp.float32)],
+        axis=1,
+    )
 
 
 def pair_terms(target, source, alive):
@@ -165,14 +274,11 @@
     return push, f_i + quad_rows(v_i, q_k), f_k + quad_rows(v_k, q_i)
 
 
-def pair_kernel(count, own_ref, all_ref, out_ref, acc_ref, tgt_ref):
+def pair_kernel(count, own_ref, near_ref, all_ref, out_ref, acc_ref, tgt_ref):
     half = count // 2
     rows = own_ref.shape[0]
     chunks = rows // LANES
     lower = my_place() < half
-    lane = lax.broadcasted_iota(jnp.int32, (8, LANES), 1)
-    sublane = lax.broadcasted_iota(jnp.int32, (8, LANES), 0)
-    diff = lane - sublane
     acc_ref[...] = jnp.zeros_like(acc_ref)
     zero = jnp.zeros((8, LANES), jnp.float32)
 
@@ -184,15 +290,6 @@
         target = [
             jnp.broadcast_to(own_ref[pl.ds(base, 8), c : c + 1], (8, LANES)) for c in range(14)
         ]
-
-        def near(chunk, sums):
-            start = pl.multiple_of(chunk * LANES, LANES)
-
-            def alive(root):
-                return jnp.where(diff == base - start, 0.0, root)
-
-            push, on_i, _ = pair_terms(target, source_at(start), alive)
-            return tuple(x + y for x, y in zip(sums, push + on_i))
 
         def far(chunk, sums):
             start = pl.multiple_of(chunk * LANES, LANES)
@@ -208,14 +305,9 @@
         def last(step, sums):
             return far(half * chunks + first + 2 * step, sums)
 
-        sums = lax.fori_loop(0, chunks, near, (zero,) * 12)
-        sums = lax.fori_loop(chunks, half * chunks, far, sums, unroll=UNROLL)
+        sums = lax.fori_loop(chunks, half * chunks, far, (zero,) * 12, unroll=UNROLL)
         sums = lax.fori_loop(0, (chunks - first + 1) // 2, last, sums)
-        tgt_ref[pl.ds(base, 8), :] = jnp.concatenate(
-            [jnp.sum(x, axis=1, keepdims=True) for x in sums]
-            + [jnp.zeros((8, LANES - 12), jnp.float32)],
-            axis=1,
-        )
+        tgt_ref[pl.ds(base, 8), :] = near_ref[pl.ds(base, 8), :] + row_sums(sums)
         return 0
 
     lax.fori_loop(0, rows // 8, one_group, 0)
@@ -333,12 +425,8 @@
     high,
     part_ref,
     both_ref,
-    dip_ref,
-    quad_ref,
-    x_out,
-    v_out,
-    f_out,
-    t_out,
+    all_ref,
+    out_ref,
     land_ref,
     force_ref,
     lo_ref,
@@ -349,7 +437,7 @@
     force_recv,
 ):
     half = count // 2
-    width = f_out.shape[1]
+    width = out_ref.shape[1]
     chunks = width // LANES
     used = 2 * chunks
     place = my_place()
@@ -446,7 +534,6 @@
 
     total = lax.fori_loop(1, half + 1, finish_one, part_ref[:, 0:width])
     force_ref[sub] = total
-    f_out[...] = total[0:3]
     swap = pltpu.make_async_remote_copy(
         src_ref=force_ref.at[sub],
         dst_ref=force_ref.at[sub],
@@ -456,10 +543,10 @@
         device_id_type=MESH,
     )
     swap.start()
-    t_out[...] = torque_of(
+    torque = torque_of(
         [total[c : c + 1] for c in range(12)],
-        [dip_ref[c : c + 1, :] for c in range(3)],
-        [quad_ref[c : c + 1, :] for c in range(6)],
+        [all_ref[c : c + 1, 0:width] for c in range(4, 7)],
+        [all_ref[c : c + 1, 0:width] for c in range(7, 13)],
     )
     swap.wait()
     v = v + (0.5 * OUTER_DT) * tiled(from_force, (0, 1, 2)) * mass
@@ -490,8 +577,7 @@
             rows.append(jnp.where(sub == 0, sides[0], sides[1]))
         return jnp.concatenate(rows, axis=0)
 
-    x_out[...] = mine(x)
-    v_out[...] = mine(v)
+    out_ref[...] = jnp.concatenate([mine(x), mine(v), total[0:3], torque], axis=0)
 
 
 def body(
@@ -509,28 +595,14 @@
 ):
     atoms = positions.shape[1]
     n_sub = lax.axis_size("sub")
-    record = jnp.concatenate(
-        [positions, charges[None, :], dipoles, quadrupoles, damping[None, :]], 0
-    )
-    padded = jnp.concatenate([record, jnp.zeros((2, atoms), jnp.float32)], 0)
-    own = padded.T
     count = lax.axis_size("blk") * lax.axis_size("rep") * n_sub
     slots = count // 2 + 1
     vmem = pl.BlockSpec(memory_space=pltpu.VMEM)
     dma = pltpu.SemaphoreType.DMA
-    indices = jnp.concatenate(
-        [bonds, angles.reshape(-1, atoms), torsions.reshape(-1, atoms)], 0
-    )
-    pack = jnp.concatenate(
-        [
-            positions,
-            velocities,
-            inverse_mass[None, :],
-            bond_length[None, :],
-            indices.astype(jnp.float32),
-        ],
-        0,
-    )
+    hbm = pl.BlockSpec(memory_space=pl.ANY)
+    scalars = jnp.stack([charges, damping, inverse_mass, bond_length])
+    index_rows = 2 + (angles.size + torsions.size) // atoms
+    pack_rows = 8 + index_rows
 
     def params(**more):
         return pltpu.CompilerParams(vmem_limit_bytes=48 * 1024 * 1024, **more)
@@ -538,19 +610,36 @@
     def shape(*dims):
         return jax.ShapeDtypeStruct(dims, jnp.float32)
 
-    everyone, both = pl.pallas_call(
+    everyone, both, own, near = pl.pallas_call(
         functools.partial(gather_kernel, count),
-        out_shape=(shape(16, slots * atoms), shape(2, *pack.shape)),
-        in_specs=[vmem] * 2,
-        out_specs=(vmem, vmem),
-        scratch_shapes=[dma((slots,)), dma((slots,)), dma, dma],
+        out_shape=(
+            shape(16, slots * atoms),
+            shape(2, pack_rows, atoms),
+            shape(atoms, LANES),
+            shape(atoms, LANES),
+        ),
+        in_specs=[hbm] * 4 + [vmem] + [hbm] * 3,
+        out_specs=(vmem,) * 4,
+        scratch_shapes=[
+            pltpu.VMEM(x.shape, x.dtype)
+            for x in (positions, velocities, dipoles, quadrupoles, bonds, angles, torsions)
+        ]
+        + [
+            pltpu.VMEM((16, atoms), jnp.float32),
+            pltpu.VMEM((pack_rows, atoms), jnp.float32),
+            dma((7,)),
+            dma((slots,)),
+            dma((slots,)),
+            dma,
+            dma,
+        ],
         compiler_params=params(collective_id=1),
         name="gather",
-    )(padded, pack)
+    )(positions, velocities, dipoles, quadrupoles, scalars, bonds, angles, torsions)
     parts = pl.pallas_call(
         functools.partial(pair_kernel, count),
         out_shape=shape(16, slots * atoms),
-        in_specs=[vmem, vmem],
+        in_specs=[vmem] * 3,
         out_specs=vmem,
         scratch_shapes=[
             pltpu.VMEM((96, slots * atoms), jnp.float32),
@@ -558,14 +647,14 @@
         ],
         compiler_params=params(),
         name="pairs",
-    )(own, everyone)
+    )(own, near, everyone)
     high = -(-(n_sub * atoms // LANES) // 8) * 8
-    total = n_sub * indices.shape[0] * atoms
-    return pl.pallas_call(
+    total = n_sub * index_rows * atoms
+    out = pl.pallas_call(
         functools.partial(final_kernel, count, high),
-        out_shape=(shape(3, atoms),) * 4,
-        in_specs=[vmem] * 4,
-        out_specs=(vmem,) * 4,
+        out_shape=shape(12, atoms),
+        in_specs=[vmem] * 3,
+        out_specs=vmem,
         scratch_shapes=[
             pltpu.VMEM((slots, 16, atoms), jnp.float32),
             pltpu.VMEM((2, 16, atoms), jnp.float32),
@@ -578,7 +667,8 @@
         ],
         compiler_params=params(collective_id=2),
         name="finale",
-    )(parts, both, dipoles, quadrupoles)
+    )(parts, both, everyone)
+    return tuple(out[3 * n : 3 * n + 3] for n in range(4))
 
 
 def solution(mesh):

time: 114 us -> 114 us (level)
  Pallas kernels: 104 us -> 106 us
  local copies, waits for them, and re-layouts: 8.16 us -> 6.16 us
    pallas_call x1, Pallas kernels: 13.8 us -> 21.8 us  [body(): pl.pallas_call(functools.partial(gather_kernel, count), out_shape=(shape(...]
    pallas_call x1, Pallas kernels: 71.3 us -> 65.2 us  [body(): pl.pallas_call(functools.partial(pair_kernel, count), out_shape=shape(16,...]
    broadcast_in_dim x5 -> x0, local copies, waits for them, and re-layouts: 2.74 us -> none  [the longest x1 0.69 us: body(): charges[None, :]]
    another operation x0 -> x4, local copies, waits for them, and re-layouts: none -> 2.07 us  [body(): scalars = jnp.stack([charges, damping, inverse_mass, bond_length])]
    unnamed x18 -> x16, local copies, waits for them, and re-layouts: 5.12 us -> 3.47 us
where the time goes in v3:
time: 114 us; the launch traced here: 113 us
  Pallas kernels  106 us (93%)
  local copies, waits for them, and re-layouts  6.16 us (5%)
    pallas_call x1, Pallas kernels, body(): pl.pallas_call(functools.partial(pair_kernel, count), out_shape=shape(16,...  65.2 us
    pallas_call x1, Pallas kernels, body(): pl.pallas_call(functools.partial(gather_kernel, count), out_shape=(shape(...  21.8 us
    pallas_call x1, Pallas kernels, body(): pl.pallas_call(functools.partial(final_kernel, count, high), out_shape=sh...  19.4 us
    unnamed x16, local copies, waits for them, and re-layouts  3.47 us

profile of v3, /device:TPU:0, one launch (start us, length us, event | category | flops | bytes accessed | tf_op | source)
XLA Modules:
  0.0 113.2 jit_solution(1370021183055052722)
XLA Ops:
  0.6 0.0 copy-start.7
  0.6 0.0 copy-start.1
  0.7 0.7 stack.15
  1.3 0.0 copy-done.7
  1.3 0.0 copy-start
  1.4 0.7 stack.17
  2.0 0.7 stack.18
  2.7 0.0 copy-done.1
  2.8 0.0 copy-done
  2.8 0.0 copy-start.2
  2.8 0.7 copy-done.2
  3.5 0.0 copy-start.3
  3.5 0.7 copy-done.3
  4.2 0.0 copy-start.4
  4.2 0.7 copy-done.4
  4.9 0.0 copy-start.5
  4.9 0.7 copy-done.5
  5.6 0.0 copy-start.6
  5.6 0.7 copy-done.6
  6.2 21.8 %gather.1 = (f32[16,3456]{1,0:T(8,128)S(1)}, f32[2,24,384]{2,1,0:T(8,128)S(1)}, f32[384,128]{1,0:T(8,128)S(1)}, f32[384,128]{1,0:T(8,128)S(1)}) custom-call(f32[3,384]{1,0:T(4,128)S(1)} %copy-done.3, f32[3,384]{1,0:T(4,128)S(1)} %copy-done.4, f32[3,384]{1,0:T(4,128)S(1)} %copy-done.5, f32[6,384]{1,0:T(8,128)S(1)} %copy-done, ...), custom_call_target="tpu_custom_call" | custom-call | tf_op jit(solution)/shard_map/gather/pallas_call | solution.py:613
  28.0 65.2 %pairs.1.part_ref = f32[16,3456]{1,0:T(8,128)S(1)} custom-call(f32[384,128]{1,0:T(8,128)S(1)} %get-tuple-element.8.own_ref, f32[384,128]{1,0:T(8,128)S(1)} %get-tuple-element.9.near_ref, f32[16,3456]{1,0:T(8,128)S(1)} %get-tuple-element.10.all_ref), custom_call_target="tpu_custom_call" | custom-call | tf_op jit(solution)/shard_map/pairs/pallas_call | solution.py:639
  93.2 19.4 %finale.1 = f32[12,384]{1,0:T(8,128)S(1)} custom-call(f32[16,3456]{1,0:T(8,128)S(1)} %pairs.1.part_ref, f32[2,24,384]{2,1,0:T(8,128)S(1)} %get-tuple-element.11.both_ref, f32[16,3456]{1,0:T(8,128)S(1)} %get-tuple-element.10.all_ref), custom_call_target="tpu_custom_call" | custom-call | tf_op jit(solution)/shard_map/finale/pallas_call | solution.py:653
  112.6 0.6 fusion
  (2 shorter events, 0.0 us)
Async XLA Ops:
  0.6 0.7 copy-start.7
  0.6 2.1 %copy-start.1 = (s32[3,768]{1,0:T(4,128)S(1)}, s32[3,768]{1,0:T(4,128)}, u32[]{:S(2)}) copy-start(s32[3,768]{1,0:T(4,128)} %angle_any.1) | copy-start | bytes 27652
  1.3 1.4 %copy-start = (f32[6,384]{1,0:T(8,128)S(1)}, f32[6,384]{1,0:T(8,128)}, u32[]{:S(2)}) copy-start(f32[6,384]{1,0:T(8,128)} %quad_any.1) | copy-start | bytes 27652
  2.8 0.7 copy-start.2
  3.5 0.7 copy-start.3
  4.2 0.7 copy-start.4
  4.9 0.7 copy-start.5
  5.6 0.7 copy-start.6

commit v4 on v3

--- a/solution.py
+++ b/solution.py
@@ -55,7 +55,10 @@
         return 0
 
     lax.fori_loop(1, half + 1, one, 0)
-    pl.semaphore_wait(barrier, 2 * half)
+
+
+def all_here(half):
+    pl.semaphore_wait(pltpu.get_barrier_semaphore(), 2 * half)
 
 
 def gather_kernel(
@@ -141,8 +144,6 @@
         copy(j).wait()
         return 0
 
-    lax.fori_loop(1, half + 1, start, 0)
-
     def cut(ref):
         whole = ref[...].astype(jnp.float32)
         return [
@@ -158,15 +159,6 @@
         + cut(torsion_ref),
         axis=0,
     )
-    swap = pltpu.make_async_remote_copy(
-        src_ref=pack_ref,
-        dst_ref=both_ref.at[sub],
-        send_sem=pack_send,
-        recv_sem=pack_recv,
-        device_id=device_at(place + 1 - 2 * sub),
-        device_id_type=MESH,
-    )
-    swap.start()
     out_ref[:, 0:width] = record_ref[...]
     both_ref[sub] = pack_ref[...]
     wide = jnp.concatenate([record_ref[...], jnp.zeros((LANES - 16, width), jnp.float32)], axis=0)
@@ -193,11 +185,25 @@
             push, on_i, _ = pair_terms(target, source, alive)
             return tuple(x + y for x, y in zip(sums, push + on_i))
 
-        sums = lax.fori_loop(0, chunks, near, (jnp.zeros((8, LANES), jnp.float32),) * 12)
+        sums = lax.fori_loop(0, chunks, near, (jnp.zeros((8, LANES), jnp.float32),) * 12, unroll=True)
         near_ref[pl.ds(base, 8), :] = row_sums(sums)
         return 0
 
-    lax.fori_loop(0, width // 8, one_group, 0)
+    groups = width // 8
+    early = groups // 3
+    lax.fori_loop(0, early, one_group, 0)
+    all_here(half)
+    lax.fori_loop(1, half + 1, start, 0)
+    swap = pltpu.make_async_remote_copy(
+        src_ref=pack_ref,
+        dst_ref=both_ref.at[sub],
+        send_sem=pack_send,
+        recv_sem=pack_recv,
+        device_id=device_at(place + 1 - 2 * sub),
+        device_id_type=MESH,
+    )
+    swap.start()
+    lax.fori_loop(early, groups, one_group, 0)
     swap.wait()
     lax.fori_loop(1, half + 1, finish_one, 0)
 
@@ -443,6 +449,7 @@
     place = my_place()
     sub = lax.axis_index("sub")
     greet(half, place, count)
+    all_here(half)
 
     def copy(j):
         return pltpu.make_async_remote_copy(
@@ -599,7 +606,7 @@
     slots = count // 2 + 1
     vmem = pl.BlockSpec(memory_space=pltpu.VMEM)
     dma = pltpu.SemaphoreType.DMA
-    hbm = pl.BlockSpec(memory_space=pl.ANY)
+    hbm = pl.BlockSpec(memory_space=pltpu.HBM)
     scalars = jnp.stack([charges, damping, inverse_mass, bond_length])
     index_rows = 2 + (angles.size + torsions.size) // atoms
     pack_rows = 8 + index_rows

time: 114 us -> 108 us (0.947)
  Pallas kernels: 106 us -> 100 us
    pallas_call x1, Pallas kernels: 21.8 us -> 15.7 us  [body(): pl.pallas_call(functools.partial(gather_kernel, count), out_shape=(shape(...]
where the time goes in v4:
time: 108 us; the launch traced here: 107 us
  Pallas kernels  100 us (93%)
  local copies, waits for them, and re-layouts  6.16 us (6%)
    pallas_call x1, Pallas kernels, body(): pl.pallas_call(functools.partial(pair_kernel, count), out_shape=shape(16,...  65.2 us
    pallas_call x1, Pallas kernels, body(): pl.pallas_call(functools.partial(final_kernel, count, high), out_shape=sh...  19.4 us
    pallas_call x1, Pallas kernels, body(): pl.pallas_call(functools.partial(gather_kernel, count), out_shape=(shape(...  15.7 us
    unnamed x16, local copies, waits for them, and re-layouts  3.47 us

profile of v4, /device:TPU:0, one launch (start us, length us, event | category | flops | bytes accessed | tf_op | source)
XLA Modules:
  0.0 107.2 jit_solution(10635127946905813953)
XLA Ops:
  0.6 0.0 copy-start.7
  0.6 0.0 copy-start.1
  0.7 0.7 stack.15
  1.3 0.0 copy-done.7
  1.3 0.0 copy-start
  1.4 0.7 stack.17
  2.0 0.7 stack.18
  2.7 0.0 copy-done.1
  2.8 0.0 copy-done
  2.8 0.0 copy-start.2
  2.8 0.7 copy-done.2
  3.5 0.0 copy-start.3
  3.5 0.7 copy-done.3
  4.2 0.0 copy-start.4
  4.2 0.7 copy-done.4
  4.9 0.0 copy-start.5
  4.9 0.7 copy-done.5
  5.6 0.0 copy-start.6
  5.6 0.7 copy-done.6
  6.2 15.7 %gather.1 = (f32[16,3456]{1,0:T(8,128)S(1)}, f32[2,24,384]{2,1,0:T(8,128)S(1)}, f32[384,128]{1,0:T(8,128)S(1)}, f32[384,128]{1,0:T(8,128)S(1)}) custom-call(f32[3,384]{1,0:T(4,128)S(1)} %copy-done.3, f32[3,384]{1,0:T(4,128)S(1)} %copy-done.4, f32[3,384]{1,0:T(4,128)S(1)} %copy-done.5, f32[6,384]{1,0:T(8,128)S(1)} %copy-done, ...), custom_call_target="tpu_custom_call" | custom-call | tf_op jit(solution)/shard_map/gather/pallas_call | solution.py:620
  22.0 65.2 %pairs.1.part_ref = f32[16,3456]{1,0:T(8,128)S(1)} custom-call(f32[384,128]{1,0:T(8,128)S(1)} %get-tuple-element.8.own_ref, f32[384,128]{1,0:T(8,128)S(1)} %get-tuple-element.9.near_ref, f32[16,3456]{1,0:T(8,128)S(1)} %get-tuple-element.10.all_ref), custom_call_target="tpu_custom_call" | custom-call | tf_op jit(solution)/shard_map/pairs/pallas_call | solution.py:646
  87.2 19.4 %finale.1 = f32[12,384]{1,0:T(8,128)S(1)} custom-call(f32[16,3456]{1,0:T(8,128)S(1)} %pairs.1.part_ref, f32[2,24,384]{2,1,0:T(8,128)S(1)} %get-tuple-element.11.both_ref, f32[16,3456]{1,0:T(8,128)S(1)} %get-tuple-element.10.all_ref), custom_call_target="tpu_custom_call" | custom-call | tf_op jit(solution)/shard_map/finale/pallas_call | solution.py:660
  106.6 0.6 fusion
  (2 shorter events, 0.0 us)
Async XLA Ops:
  0.6 0.7 copy-start.7
  0.6 2.1 %copy-start.1 = (s32[3,768]{1,0:T(4,128)S(1)}, s32[3,768]{1,0:T(4,128)}, u32[]{:S(2)}) copy-start(s32[3,768]{1,0:T(4,128)} %angle_any.1) | copy-start | bytes 27652
  1.3 1.4 %copy-start = (f32[6,384]{1,0:T(8,128)S(1)}, f32[6,384]{1,0:T(8,128)}, u32[]{:S(2)}) copy-start(f32[6,384]{1,0:T(8,128)} %quad_any.1) | copy-start | bytes 27652
  2.8 0.7 copy-start.2
  3.5 0.7 copy-start.3
  4.2 0.7 copy-start.4
  4.9 0.7 copy-start.5
  5.6 0.7 copy-start.6

commit v5 on v4

--- a/solution.py
+++ b/solution.py
@@ -16,7 +16,7 @@
 ANGLE_REST = -0.33
 TORSION_K = 2.0
 OUTER_DT = 0.2
-UNROLL = 3
+UNROLL = 7
 
 
 def dot3(left, right):
@@ -449,7 +449,6 @@
     place = my_place()
     sub = lax.axis_index("sub")
     greet(half, place, count)
-    all_here(half)
 
     def copy(j):
         return pltpu.make_async_remote_copy(
@@ -468,8 +467,6 @@
     def finish_one(j, total):
         copy(j).wait()
         return total + land_ref[j]
-
-    lax.fori_loop(1, half + 1, start, 0)
 
     rows = both_ref.shape[1]
     n_mult = (rows - 10) // 7
@@ -504,6 +501,8 @@
         return force_ref[k, row : row + 1, at : at + LANES]
 
     mass = tiled(from_pack, (6, 6, 6))
+    all_here(half)
+    lax.fori_loop(1, half + 1, start, 0)
 
     def push_at(coords):
         looked = merge3(

time: 108 us -> 107 us (level)
  no operation moved by 1% of the time
where the time goes in v5:
time: 107 us; the launch traced here: 106 us
  Pallas kernels  99.6 us (93%)
  local copies, waits for them, and re-layouts  6.16 us (6%)
    pallas_call x1, Pallas kernels, body(): pl.pallas_call(functools.partial(pair_kernel, count), out_shape=shape(16,...  64.5 us
    pallas_call x1, Pallas kernels, body(): pl.pallas_call(functools.partial(final_kernel, count, high), out_shape=sh...  19.4 us
    pallas_call x1, Pallas kernels, body(): pl.pallas_call(functools.partial(gather_kernel, count), out_shape=(shape(...  15.7 us
    unnamed x16, local copies, waits for them, and re-layouts  3.47 us

profile of v5, /device:TPU:0, one launch (start us, length us, event | category | flops | bytes accessed | tf_op | source)
XLA Modules:
  0.0 106.5 jit_solution(13717509887925546496)
XLA Ops:
  0.6 0.0 copy-start.7
  0.6 0.0 copy-start.1
  0.7 0.7 stack.15
  1.3 0.0 copy-done.7
  1.3 0.0 copy-start
  1.4 0.7 stack.17
  2.0 0.7 stack.18
  2.7 0.0 copy-done.1
  2.8 0.0 copy-done
  2.8 0.0 copy-start.2
  2.8 0.7 copy-done.2
  3.5 0.0 copy-start.3
  3.5 0.7 copy-done.3
  4.2 0.0 copy-start.4
  4.2 0.7 copy-done.4
  4.9 0.0 copy-start.5
  4.9 0.7 copy-done.5
  5.6 0.0 copy-start.6
  5.6 0.7 copy-done.6
  6.2 15.7 %gather.1 = (f32[16,3456]{1,0:T(8,128)S(1)}, f32[2,24,384]{2,1,0:T(8,128)S(1)}, f32[384,128]{1,0:T(8,128)S(1)}, f32[384,128]{1,0:T(8,128)S(1)}) custom-call(f32[3,384]{1,0:T(4,128)S(1)} %copy-done.3, f32[3,384]{1,0:T(4,128)S(1)} %copy-done.4, f32[3,384]{1,0:T(4,128)S(1)} %copy-done.5, f32[6,384]{1,0:T(8,128)S(1)} %copy-done, ...), custom_call_target="tpu_custom_call" | custom-call | tf_op jit(solution)/shard_map/gather/pallas_call | solution.py:619
  22.0 64.5 %pairs.1.part_ref = f32[16,3456]{1,0:T(8,128)S(1)} custom-call(f32[384,128]{1,0:T(8,128)S(1)} %get-tuple-element.8.own_ref, f32[384,128]{1,0:T(8,128)S(1)} %get-tuple-element.9.near_ref, f32[16,3456]{1,0:T(8,128)S(1)} %get-tuple-element.10.all_ref), custom_call_target="tpu_custom_call" | custom-call | tf_op jit(solution)/shard_map/pairs/pallas_call | solution.py:645
  86.5 19.4 %finale.1 = f32[12,384]{1,0:T(8,128)S(1)} custom-call(f32[16,3456]{1,0:T(8,128)S(1)} %pairs.1.part_ref, f32[2,24,384]{2,1,0:T(8,128)S(1)} %get-tuple-element.11.both_ref, f32[16,3456]{1,0:T(8,128)S(1)} %get-tuple-element.10.all_ref), custom_call_target="tpu_custom_call" | custom-call | tf_op jit(solution)/shard_map/finale/pallas_call | solution.py:659
  105.9 0.6 fusion
  (2 shorter events, 0.0 us)
Async XLA Ops:
  0.6 0.7 copy-start.7
  0.6 2.1 %copy-start.1 = (s32[3,768]{1,0:T(4,128)S(1)}, s32[3,768]{1,0:T(4,128)}, u32[]{:S(2)}) copy-start(s32[3,768]{1,0:T(4,128)} %angle_any.1) | copy-start | bytes 27652
  1.3 1.4 %copy-start = (f32[6,384]{1,0:T(8,128)S(1)}, f32[6,384]{1,0:T(8,128)}, u32[]{:S(2)}) copy-start(f32[6,384]{1,0:T(8,128)} %quad_any.1) | copy-start | bytes 27652
  2.8 0.7 copy-start.2
  3.5 0.7 copy-start.3
  4.2 0.7 copy-start.4
  4.9 0.7 copy-start.5
  5.6 0.7 copy-start.6
